TPU v7x, 32 devices: a whole 2x2x4 slice. The times are simulated.
32 devices in a mesh: segment: 4 (over y, x), tile: 8 (over z, core).
Axes of the slice: x: 2, y: 2, z: 4, core: 2. Of those that a mesh axis runs over, the one named last changes fastest.
Arguments:
- raw_frames: bfloat16 [32, 1280, 1280], P(('segment', 'tile')), may hold values from -6 to 6
- dark_frame: bfloat16 [1280, 1280], replicated, may hold values from -2.5 to 2.5
- flat_field: bfloat16 [1280, 1280], replicated, may hold values from 0.25 to 1.75
- seeing: float32 [32, 64], P(None, 'tile'), may hold values from 0.1 to 10
- anchors: int32 [64, 2], replicated, may hold values from 0 to 1023, as said below
- taper: int32 [64], replicated, may hold values from 16 to 64
Outputs:
- power: float32 [64, 256, 256], P('tile', 'segment')
- cross: float32 [64, 4, 256, 256], P('tile', None, 'segment')
Inputs may be any that keep to these rules, and one draw needn't show every extreme that they name: `anchors`: the subfield g = 8 i + j has anchor (128 i + a, 128 j + b) with a and b below 128.
All inputs are finite; a program needn't handle non-finite values.
Results may differ from a plain program's by a relative error of at most 0.013.
Values may be sent and summed in bfloat16 or wider, within the bound.
No kernel may reach another device: no remote copies, remote signals or barrier semaphores. Data moves between devices by JAX's collectives and lax.ppermute only.
A program may use at most 192 MiB of HBM per device.

v0:
```python
import math

import jax
import jax.numpy as jnp
from jax import lax
from jax.sharding import PartitionSpec as P

S = 256


def ramp_rows(taper, size):
    place = jnp.arange(size, dtype=jnp.float32)[None, :]
    width = taper.astype(jnp.float32)[:, None]
    left = jnp.where(place < width, 0.5 - 0.5 * jnp.cos(jnp.pi * (place + 0.5) / width), 1.0)
    return left * left[:, ::-1]


def dft_tables(size):
    steps = jnp.arange(size, dtype=jnp.int32)
    phase = steps[:, None] * steps[None, :] % size
    angle = 2.0 * jnp.pi * phase.astype(jnp.float32) / size
    factor = 1.0 / jnp.sqrt(jnp.float32(size))
    return (
        (jnp.cos(angle) * factor).astype(jnp.bfloat16),
        (jnp.sin(angle) * factor).astype(jnp.bfloat16),
    )


def first_pass(sub, cosine, sine):
    table = jnp.concatenate([cosine, -sine], axis=1)
    return jnp.einsum("fsxy,yk->fsxk", sub, table, preferred_element_type=jnp.float32).astype(
        jnp.bfloat16
    )


def second_pass(half, cosine, sine):
    size = cosine.shape[0]
    with_cos = jnp.einsum("ux,fsxk->fsuk", cosine, half, preferred_element_type=jnp.float32)
    with_sin = jnp.einsum("ux,fsxk->fsuk", sine, half, preferred_element_type=jnp.float32)
    real_part = with_cos[..., :size] + with_sin[..., size:]
    imag_part = with_cos[..., size:] - with_sin[..., :size]
    return (real_part, imag_part)


def local(raw_frames, dark_frame, flat_field, seeing, anchors, taper):
    size = S
    cosine, sine = dft_tables(size)
    ramps = ramp_rows(taper, size)
    calibrated = (
        raw_frames.astype(jnp.float32) - dark_frame.astype(jnp.float32)[None]
    ) / flat_field.astype(jnp.float32)[None]

    def cutout(anchor, ramp):
        start = jnp.zeros((), jnp.int32)
        cal = lax.dynamic_slice(
            calibrated, (start, anchor[0], anchor[1]), (calibrated.shape[0], size, size)
        )
        centered = cal - jnp.mean(cal, axis=(1, 2), keepdims=True)
        return (centered * (ramp[:, None] * ramp[None, :])[None]).astype(jnp.bfloat16)

    sub = jax.vmap(cutout, in_axes=(0, 0), out_axes=1)(anchors, ramps)
    received = lax.all_to_all(sub, "tile", split_axis=1, concat_axis=0, tiled=True)
    n_frames = received.shape[0]
    sub_dev = received.shape[1]
    block = math.gcd(n_frames, 8)
    n_blocks = n_frames // block
    segment_index = lax.axis_index("segment")
    weights = lax.dynamic_slice_in_dim(seeing, segment_index * n_frames, n_frames, 0)
    weight_sum = jnp.sum(seeing, axis=0)
    blocks = received.reshape((n_blocks, block) + received.shape[1:])
    weight_blocks = weights.reshape(n_blocks, block, sub_dev)

    def accumulate(carry, inputs):
        data, wblock = inputs
        half = first_pass(data, cosine, sine)
        real_part, imag_part = second_pass(half, cosine, sine)
        wgt = wblock[:, :, None, None]
        power_sum = carry[0] + jnp.sum(
            wgt * (real_part * real_part + imag_part * imag_part), axis=0
        )
        real_u = jnp.roll(real_part, -1, axis=2)
        imag_u = jnp.roll(imag_part, -1, axis=2)
        real_v = jnp.roll(real_part, -1, axis=3)
        imag_v = jnp.roll(imag_part, -1, axis=3)
        cross_sum = carry[1] + jnp.stack(
            [
                jnp.sum(wgt * (real_part * real_u + imag_part * imag_u), axis=0),
                jnp.sum(wgt * (imag_part * real_u - real_part * imag_u), axis=0),
                jnp.sum(wgt * (real_part * real_v + imag_part * imag_v), axis=0),
                jnp.sum(wgt * (imag_part * real_v - real_part * imag_v), axis=0),
            ],
            axis=1,
        )
        return ((power_sum, cross_sum), None)

    start_power = jnp.zeros((sub_dev, size, size), jnp.float32)
    start_cross = jnp.zeros((sub_dev, 4, size, size), jnp.float32)
    (power_sum, cross_sum), unused = lax.scan(
        accumulate, (start_power, start_cross), (blocks, weight_blocks)
    )
    power_rows, cross_rows = (
        lax.psum_scatter(
            power_sum.astype(jnp.bfloat16), "segment", scatter_dimension=1, tiled=True
        ).astype(jnp.float32),
        lax.psum_scatter(
            cross_sum.astype(jnp.bfloat16), "segment", scatter_dimension=2, tiled=True
        ).astype(jnp.float32),
    )
    power = power_rows / weight_sum[:, None, None]
    cross = cross_rows / weight_sum[:, None, None, None]
    return (power, cross)


def solution(mesh):
    placed = (P(("segment", "tile"), None, None), P(), P(), P(None, "tile"), P(), P())
    return jax.shard_map(
        local,
        mesh=mesh,
        in_specs=placed,
        out_specs=(P("tile", "segment", None), P("tile", None, "segment", None)),
        check_vma=False,
    )
```

profile of v0, /device:TPU:0, one launch (start us, length us, event | category | flops | bytes accessed | tf_op | source)
XLA Modules:
  0.0 746.0 jit_solution(13757384058877534190)
XLA Ops:
  9.4 7.9 %convert_divide_fusion = f32[1,1280,1280]{2,1,0:T(8,128)} fusion(bf16[1,1280,1280]{2,1,0:T(8,128)(2,1)} %param.6, bf16[1280,1280]{1,0:T(8,128)(2,1)} %param.8, bf16[1280,1280]{1,0:T(8,128)(2,1)} %param.7), kind=kLoop, calls=%fused_computation.19 | loop fusion | flops 8192000 | bytes 16384000 | tf_op jit(solution)/shard_map/div | solution.py:49
  17.3 242.0 %while.1 = (s32[]{:T(128)}, f32[1,1280,1280]{2,1,0:T(8,128)}, s32[64,3]{0,1:T(4,128)S(1)}, f32[64,1,256,256]{3,2,1,0:T(8,128)}, s32[]{:T(128)}) while((s32[]{:T(128)}, f32[1,1280,1280]{2,1,0:T(8,128)}, s32[64,3]{0,1:T(4,128)S(1)}, f32[64,1,256,256]{3,2,1,0:T(8,128)}, s32[]{:T(128)}) %tuple.34), condition=%wide.while_cond, body=%wide.while_body.sunk | while | flops 2 | bytes 525929 | solution.py:55
  48.2 3.1 bitcast_dynamic-update-slice_fusion.2
  146.5 3.1 bitcast_dynamic-update-slice_fusion.2
  150.3 3.1 bitcast_dynamic-update-slice_fusion.2
  259.3 7.0 reduce_sum.68
  266.3 9.7 %fusion.1 = bf16[1,64,256,256]{3,2,0,1:T(8,128)(2,1)} fusion(f32[64,1,256,256]{3,2,1,0:T(8,128)} %get-tuple-element.30, f32[64,256]{1,0:T(8,128)S(1)} %fusion.16, f32[64]{0:T(128)S(1)} %broadcast_multiply_fusion), kind=kLoop, calls=%fused_computation.10 | loop fusion | flops 16777216 | bytes 25231616 | tf_op jit(solution)/shard_map/vmap()/convert_element_type | solution.py:59
  276.0 6.3 all-to-all-start
  284.5 181.8 %all-to-all-done = bf16[1,64,256,256]{3,2,0,1:T(8,128)(2,1)} async-done(((bf16[1,64,256,256]{3,2,0,1:T(8,128)(2,1)}), bf16[1,64,256,256]{3,2,0,1:T(8,128)(2,1)}, u32[]{:S(2)}, u32[]{:S(2)}) %all-to-all-start) | async-done | bytes 8388640 | tf_op jit(solution)/shard_map/all_to_all | solution.py:62
  466.3 11.6 %convolution_convert_fusion = bf16[8,8,256,512]{3,2,1,0:T(8,128)(2,1)} fusion(bf16[8,8,256,256]{3,2,1,0:T(8,128)(2,1)} %bitcast.3, bf16[256,256]{1,0:T(8,128)(2,1)S(1)} %fusion.12, bf16[256,256]{1,0:T(8,128)(2,1)S(1)} %multiply_convert_fusion.1), kind=kOutput, calls=%fused_computation.18 | convolution fusion | flops 4303880192 | bytes 25427968 | tf_op jit(solution)/shard_map/while/body/eval_jaxpr/fsxy,yk->fsxk/dot_general | solution.py:31
  477.9 22.3 %convolution_bitcast_fusion = f32[8,8,256,512]{2,3,1,0:T(8,128)} fusion(bf16[8,8,256,512]{3,2,1,0:T(8,128)(2,1)} %convolution_convert_fusion), kind=kOutput, calls=%fused_computation.16 | convolution fusion | flops 4296015872 | bytes 50331648 | tf_op jit(solution)/shard_map/while/body/eval_jaxpr/ux,fsxk->fsuk/dot_general | solution.py:39
  500.3 22.3 %convolution_bitcast_fusion.1 = f32[8,8,256,512]{2,3,1,0:T(8,128)} fusion(bf16[8,8,256,512]{3,2,1,0:T(8,128)(2,1)} %convolution_convert_fusion), kind=kOutput, calls=%fused_computation.17 | convolution fusion | flops 4296015872 | bytes 50331648 | tf_op jit(solution)/shard_map/while/body/eval_jaxpr/ux,fsxk->fsuk/dot_general | solution.py:38
  522.6 34.0 %slice_add_fusion = (f32[8,8,256,256]{2,3,1,0:T(8,128)}, f32[8,8,256,256]{2,3,1,0:T(8,128)}) fusion(f32[8,8,256,512]{2,3,1,0:T(8,128)} %convolution_bitcast_fusion, f32[8,8,256,512]{2,3,1,0:T(8,128)} %convolution_bitcast_fusion.1), kind=kLoop, calls=%fused_computation.3 | loop fusion | flops 8388608 | bytes 100663296 | tf_op jit(solution)/shard_map/while/body/eval_jaxpr/add | solution.py:40
  556.6 15.4 %slice.91 = f32[8,8,255,256]{2,3,1,0:T(8,128)} slice(f32[8,8,256,256]{2,3,1,0:T(8,128)} %get-tuple-element.52), slice={[0:8], [0:8], [1:256], [0:256]} | slice | bytes 33423360 | tf_op jit(solution)/shard_map/while/body/eval_jaxpr/jit(_roll_static)/slice | solution.py:81
  573.1 8.5 %slice.95 = f32[8,8,256,255]{2,3,1,0:T(8,128)} slice(f32[8,8,256,256]{2,3,1,0:T(8,128)S(1)} %copy-done), slice={[0:8], [0:8], [0:256], [1:256]} | slice | bytes 33423360 | tf_op jit(solution)/shard_map/while/body/eval_jaxpr/jit(_roll_static)/slice | solution.py:83
  583.8 7.5 %slice.93 = f32[8,8,255,256]{2,3,1,0:T(8,128)} slice(f32[8,8,256,256]{2,3,1,0:T(8,128)S(1)} %bitcast.58), slice={[0:8], [0:8], [1:256], [0:256]} | slice | bytes 33423360 | tf_op jit(solution)/shard_map/while/body/eval_jaxpr/jit(_roll_static)/slice | solution.py:82
  591.3 6.5 slice.97
  597.7 4.0 slice.92
  601.7 7.7 %slice.94 = f32[8,8,1,256]{2,3,1,0:T(8,128)} slice(f32[8,8,256,256]{2,3,1,0:T(8,128)} %get-tuple-element.53), slice={[0:8], [0:8], [0:1], [0:256]} | slice | bytes 131072 | tf_op jit(solution)/shard_map/while/body/eval_jaxpr/jit(_roll_static)/slice | solution.py:82
  610.5 39.9 %multiply_reduce_fusion.3 = (bf16[8,256,256]{1,2,0:T(8,128)(2,1)S(1)}, bf16[8,256,256]{1,2,0:T(8,128)(2,1)S(1)}, bf16[8,256,256]{1,2,0:T(8,128)(2,1)}, bf16[8,256,256]{1,2,0:T(8,128)(2,1)}, bf16[8,256,256]{1,2,0:T(8,128)(2,1)S(1)}) fusion(f32[8,8,256,256]{2,3,1,0:T(8,128)} %get-tuple-element.53, f32[8,8,256,256]{2,3,1,0:T(8,128)} %get-tuple-element.52, ...), kind=kLoop, calls=%fused_computation.14 | loop fusion | flops 119013376 | bytes 105906432 | tf_op jit(solution)/shard_map/while/body/eval_jaxpr/reduce_sum | solution.py:87
  652.3 3.7 pad_maximum_fusion.4
  656.0 8.0 %copy.20 = bf16[8,4,256,256]{3,0,1,2:T(8,128)(2,1)} copy(bf16[8,4,256,256]{2,3,0,1:T(8,128)(2,1)} %pad_maximum_fusion.4) | data formatting | bytes 8388608 | tf_op jit(solution)/shard_map/while/body/eval_jaxpr/stack | solution.py:85
  664.1 14.9 %reduce-scatter.3.cloned.1.call-done = bf16[8,64,256]{2,0,1:T(8,128)(2,1)} async-done(((bf16[8,256,256]{2,0,1:T(8,128)(2,1)}), bf16[8,64,256]{2,0,1:T(8,128)(2,1)}) %reduce-scatter.3.cloned.1.call-update) | async-done | bytes 262160 | tf_op jit(solution)/shard_map/reduce_scatter | solution.py:102
  681.1 54.0 %reduce-scatter.5.cloned.1.call-done = bf16[8,4,64,256]{3,0,1,2:T(8,128)(2,1)} async-done(((bf16[8,4,256,256]{3,0,1,2:T(8,128)(2,1)}), bf16[8,4,64,256]{3,0,1,2:T(8,128)(2,1)}) %reduce-scatter.5.cloned.1.call-update) | async-done | bytes 1048592 | tf_op jit(solution)/shard_map/reduce_scatter | solution.py:105
  (230 shorter events, 249.6 us)
Async XLA Ops:
  266.3 16.1 %copy-start.1 = (f32[32,8]{0,1:T(8,128)S(1)}, f32[32,8]{0,1:T(8,128)}, u32[]{:S(2)}) copy-start(f32[32,8]{0,1:T(8,128)} %param.9) | copy-start | bytes 3076
  276.0 190.3 %all-to-all-start = ((bf16[1,64,256,256]{3,2,0,1:T(8,128)(2,1)}), bf16[1,64,256,256]{3,2,0,1:T(8,128)(2,1)}, u32[]{:S(2)}, u32[]{:S(2)}) async-start(bf16[1,64,256,256]{3,2,0,1:T(8,128)(2,1)} %fusion.1), calls=%async_computation | async-start | bytes 16777216 | tf_op jit(solution)/shard_map/all_to_all | solution.py:62
  282.3 396.7 %reduce-scatter.3.cloned.1.call-start = ((), (), s32[]{:S(2)}) async-start(), calls=%async_computation.3 | async-start | bytes 1310720 | tf_op jit(solution)/shard_map/reduce_scatter | solution.py:102
  556.6 16.5 %copy-start = (f32[8,8,256,256]{2,3,1,0:T(8,128)S(1)}, f32[8,8,256,256]{2,3,1,0:T(8,128)}, u32[]{:S(2)}) copy-start(f32[8,8,256,256]{2,3,1,0:T(8,128)} %get-tuple-element.52) | copy-start | bytes 50331652
  556.6 25.0 %slice-start = ((s8[16777216]{0:T(1024)(128)(4,1)}), s8[4194304]{0:T(1024)(128)(4,1)S(1)}, s32[]{:S(2)}) async-start(s8[16777216]{0:T(1024)(128)(4,1)} %bitcast.57), calls=%async_computation.5 | async-start | bytes 8388608
  556.6 25.0 %slice-start.1 = ((s8[16777216]{0:T(1024)(128)(4,1)}), s8[4194304]{0:T(1024)(128)(4,1)S(1)}, s32[]{:S(2)}) async-start(s8[16777216]{0:T(1024)(128)(4,1)} %bitcast.57), calls=%async_computation.6 | async-start | bytes 8388608
  573.1 9.1 %slice-start.2 = ((s8[16777216]{0:T(1024)(128)(4,1)}), s8[4194304]{0:T(1024)(128)(4,1)S(1)}, s32[]{:S(2)}) async-start(s8[16777216]{0:T(1024)(128)(4,1)} %bitcast.57), calls=%async_computation.7 | async-start | bytes 8388608
  573.1 10.7 %slice-start.3 = ((s8[16777216]{0:T(1024)(128)(4,1)}), s8[4194304]{0:T(1024)(128)(4,1)S(1)}, s32[]{:S(2)}) async-start(s8[16777216]{0:T(1024)(128)(4,1)} %bitcast.57), calls=%async_computation.8 | async-start | bytes 8388608
  650.4 13.6 %copy-start.2 = (f32[32,8]{0,1:T(8,128)S(1)}, f32[32,8]{0,1:T(8,128)}, u32[]{:S(2)}) copy-start(f32[32,8]{0,1:T(8,128)} %param.9) | copy-start | bytes 3076
  652.2 82.8 %reduce-scatter.5.cloned.1.call-start = ((), (), s32[]{:S(2)}) async-start(), calls=%async_computation.4 | async-start | bytes 5242880 | tf_op jit(solution)/shard_map/reduce_scatter | solution.py:105
Sparse Core Ops, SparseCore 0:
  652.4 26.6 reduce-scatter.2
  682.3 52.6 reduce-scatter.4
where the time goes:
time: 752 us; the launch traced here: 746 us
  local copies, waits for them, and re-layouts  309 us (41%)
  waiting for transfers between devices  251 us (33%)
  other arithmetic  109 us (14%)
  matrix products  56.3 us (7%)
  between operations  14.1 us (2%)
    gather x192, local copies, waits for them, and re-layouts  242 us
    all_to_all x1, waiting for transfers between devices, local(): lax.all_to_all(sub, 'tile', split_axis=1, concat_axis=0, tiled=True)  182 us
    reduce_scatter x1, waiting for transfers between devices, local(): lax.psum_scatter(cross_sum.astype(jnp.bfloat16), 'segment', scatter_dimen...  54 us
    reduce_sum x1, other arithmetic, accumulate(): jnp.sum(wgt * (real_part * real_u + imag_part * imag_u), axis=0)  39.9 us
    add x1, other arithmetic, second_pass(): real_part = with_cos[..., :size] + with_sin[..., size:]  34 us
    dot_general x1, matrix products, second_pass(): jnp.einsum('ux,fsxk->fsuk', sine, half, preferred_element_type=jnp.float32)  22.3 us
    dot_general x1, matrix products, second_pass(): jnp.einsum('ux,fsxk->fsuk', cosine, half, preferred_element_type=jnp.floa...  22.3 us
    slice x2, local copies, waits for them, and re-layouts, accumulate(): real_u = jnp.roll(real_part, -1, axis=2)  19.3 us
  transfers between devices with their start and end apart: 3, of which 3 were waited for; matrix products, arithmetic and copies ran while one was open for 2% of the time, Pallas kernels for 0%

commit v1 on v0

--- a/solution.py
+++ b/solution.py
@@ -3,9 +3,15 @@
 import jax
 import jax.numpy as jnp
 from jax import lax
+from jax.experimental import pallas as pl
+from jax.experimental.pallas import tpu as pltpu
 from jax.sharding import PartitionSpec as P
 
 S = 256
+GROUP = 256
+REGION = 384
+HALF = 136
+VMEM_LIMIT = 60000 * 1024
 
 
 def ramp_rows(taper, size):
@@ -42,7 +48,7 @@
     return (real_part, imag_part)
 
 
-def local(raw_frames, dark_frame, flat_field, seeing, anchors, taper):
+def local_any(raw_frames, dark_frame, flat_field, seeing, anchors, taper):
     size = S
     cosine, sine = dft_tables(size)
     ramps = ramp_rows(taper, size)
@@ -111,10 +117,307 @@
     return (power, cross)
 
 
+def shifted_ramps(taper, offset, length):
+    place = jnp.arange(length, dtype=jnp.int32)[None, :] - offset[:, None]
+    inside = (place >= 0) & (place < S)
+    width = taper.astype(jnp.float32)[:, None]
+
+    def side(spot):
+        spot = spot.astype(jnp.float32)
+        rise = 0.5 - 0.5 * jnp.cos(jnp.pi * (spot + 0.5) / width)
+        return jnp.where(spot < width, rise, 1.0)
+
+    return jnp.where(inside, side(place) * side(S - 1 - place), 0.0)
+
+
+def spectra_kernel(
+    scal, wgt, own0, own1, far0, far1, dark0, dark1, rate0, rate1, ramp, wave, table, out,
+    cal, shifted, real, imag, sums,
+):
+    step = pl.program_id(0)
+    pair = ramp.shape[0]
+    segment = scal[0]
+
+    @pl.when(step == 0)
+    def _():
+        sums[...] = jnp.zeros_like(sums)
+        for j in range(pair):
+            first = 128 - scal[4 + 2 * j + 1]
+            for m in range(4):
+                shifted[j, :, 128 * m : 128 * m + 128] = wave[m, pl.ds(first, REGION), :].astype(
+                    jnp.bfloat16
+                )
+
+    lane = lax.broadcasted_iota(jnp.int32, (1, 128), 1)
+    last_lane = lax.broadcasted_iota(jnp.int32, (8, 128), 1) == 127
+    for near in range(2):
+        for m in range(4):
+            left = (own0, far0)[near] if m < 2 else (own1, far1)[near]
+            dark = dark0 if m < 2 else dark1
+            rate = rate0 if m < 2 else rate1
+            cols = slice(128 * (m % 2), 128 * (m % 2) + 128)
+            cal[near, m] = (left[0, :, cols].astype(jnp.float32) - dark[:, cols]) * rate[:, cols]
+    for near in range(2):
+        frame = scal[1] + 2 * step + (scal[2] if near == 0 else 1 - scal[2])
+        for j in range(pair):
+            top = scal[4 + 2 * j]
+            left = scal[4 + 2 * j + 1]
+            weight = wgt[frame, scal[3] + j]
+            pieces = [cal[near, j + m, pl.ds(top, S), :] for m in range(3)]
+            total = [jnp.sum(piece, axis=0, keepdims=True) for piece in pieces]
+            total = (
+                jnp.where(lane >= left, total[0], 0.0)
+                + total[1]
+                + jnp.where(lane < left, total[2], 0.0)
+            )
+            mean = jnp.sum(total, axis=1, keepdims=True) * (1.0 / (S * S))
+            sub = jnp.concatenate(
+                [
+                    ((piece - mean) * ramp[j, :, 128 * m : 128 * m + 128]).astype(jnp.bfloat16)
+                    for m, piece in enumerate(pieces)
+                ],
+                axis=1,
+            )
+            half = jnp.dot(sub, shifted[j], preferred_element_type=jnp.float32).astype(jnp.bfloat16)
+            both = jnp.dot(table[...], half, preferred_element_type=jnp.float32)
+            for m in range(2):
+                lo = slice(128 * m, 128 * m + 128)
+                hi = slice(S + 128 * m, S + 128 * m + 128)
+                real[near, j, m] = both[:HALF, lo] + both[HALF:, hi]
+                imag[near, j, m] = both[:HALF, hi] - both[HALF:, lo]
+            for r in range(0, HALF, 8):
+                rows = slice(r, r + 8)
+                re = [real[near, j, m, rows, :] for m in range(2)]
+                im = [imag[near, j, m, rows, :] for m in range(2)]
+                re_s = [pltpu.roll(x, 127, 1) for x in re]
+                im_s = [pltpu.roll(x, 127, 1) for x in im]
+                for m in range(2):
+                    wre = re[m] * weight
+                    wim = im[m] * weight
+                    sums[j, 0, m, rows, :] += wre * re[m] + wim * im[m]
+                    if r < 128:
+                        below = slice(r + 1, r + 9)
+                        re_u = real[near, j, m, below, :]
+                        im_u = imag[near, j, m, below, :]
+                        sums[j, 1, m, rows, :] += wre * re_u + wim * im_u
+                        sums[j, 2, m, rows, :] += wim * re_u - wre * im_u
+                    re_v = jnp.where(last_lane, re_s[1 - m], re_s[m])
+                    im_v = jnp.where(last_lane, im_s[1 - m], im_s[m])
+                    sums[j, 3, m, rows, :] += wre * re_v + wim * im_v
+                    sums[j, 4, m, rows, :] += wim * re_v - wre * im_v
+
+    @pl.when(step == pl.num_programs(0) - 1)
+    def _():
+        for target in range(4):
+            slot = jnp.bitwise_xor(segment, target)
+            for j in range(pair):
+                for plane in range(5):
+                    first = (0, 64, 64, 0)[target]
+                    if plane not in (1, 2):
+                        first = (0, 64, 65, 1)[target]
+                    for m in range(2):
+                        out[slot, j, plane, :, 128 * m : 128 * m + 128] = sums[
+                            j, plane, m, first : first + 64, :
+                        ].astype(jnp.bfloat16)
+
+
+def spectra(p, scal, seeing, own, far, dark, rate, ramp, wave, table):
+    n = own[0].shape[0]
+    frames = pl.BlockSpec((1, REGION, GROUP), lambda i, s: (i, 0, 0))
+    left = pl.BlockSpec((REGION, GROUP), lambda i, s: (0, p))
+    right = pl.BlockSpec((REGION, GROUP), lambda i, s: (0, p + 1))
+    return pl.pallas_call(
+        spectra_kernel,
+        name="spectra",
+        grid_spec=pltpu.PrefetchScalarGridSpec(
+            num_scalar_prefetch=1,
+            grid=(n,),
+            in_specs=[
+                pl.BlockSpec(memory_space=pltpu.SMEM),
+                frames,
+                frames,
+                frames,
+                frames,
+                left,
+                right,
+                left,
+                right,
+                pl.BlockSpec((2, S, REGION), lambda i, s: (p, 0, 0)),
+                pl.BlockSpec(wave.shape, lambda i, s: (0, 0, 0)),
+                pl.BlockSpec(table.shape, lambda i, s: (0, 0)),
+            ],
+            out_specs=pl.BlockSpec((4, 2, 5, 64, S), lambda i, s: (0, 0, 0, 0, 0)),
+            scratch_shapes=[
+                pltpu.VMEM((2, 4, REGION, 128), jnp.float32),
+                pltpu.VMEM((2, REGION, 2 * S), jnp.bfloat16),
+                pltpu.VMEM((2, 2, 2, HALF, 128), jnp.float32),
+                pltpu.VMEM((2, 2, 2, HALF, 128), jnp.float32),
+                pltpu.VMEM((2, 5, 2, HALF, 128), jnp.float32),
+            ],
+        ),
+        out_shape=jax.ShapeDtypeStruct((4, 2, 5, 64, S), jnp.bfloat16),
+        compiler_params=pltpu.CompilerParams(
+            dimension_semantics=("arbitrary",), vmem_limit_bytes=VMEM_LIMIT
+        ),
+    )(scal, seeing, own[0], own[1], far[0], far[1], dark, dark, rate, rate, ramp, wave, table)
+
+
+def finish_kernel(mine, got1, got2, got3, flip, mix, inverse, *refs):
+    power, cross = refs[-2:]
+    for j in range(2):
+        for plane in range(5):
+            parts = jnp.concatenate([x[0, j, plane] for x in (mine, got1, got2, got3)], axis=0)
+            turned = jnp.dot(
+                parts, flip[1 if plane >= 3 else 0], preferred_element_type=jnp.float32
+            ).astype(jnp.bfloat16)
+            total = jnp.dot(mix[...], turned, preferred_element_type=jnp.float32)
+            total = total * inverse[j]
+            if plane == 0:
+                power[j] = total
+            else:
+                cross[j, plane - 1] = total
+
+
+def finish(p, parts, flip, mix, inverse, before, n_sub):
+    part = pl.BlockSpec((1, 2, 5, 64, S), lambda i: (0, 0, 0, 0, 0))
+    specs = [part] * 4 + [
+        pl.BlockSpec((2, S, S), lambda i: (0, 0, 0)),
+        pl.BlockSpec((64, S), lambda i: (0, 0)),
+        pl.BlockSpec((2, 1, S), lambda i: (p, 0, 0)),
+    ]
+    aliases = {}
+    if before is not None:
+        specs += [pl.BlockSpec(memory_space=pl.ANY)] * 2
+        aliases = {7: 0, 8: 1}
+    return pl.pallas_call(
+        finish_kernel,
+        name="finish",
+        grid=(1,),
+        in_specs=specs,
+        out_specs=[
+            pl.BlockSpec((2, 64, S), lambda i: (p, 0, 0)),
+            pl.BlockSpec((2, 4, 64, S), lambda i: (p, 0, 0, 0)),
+        ],
+        out_shape=[
+            jax.ShapeDtypeStruct((n_sub, 64, S), jnp.float32),
+            jax.ShapeDtypeStruct((n_sub, 4, 64, S), jnp.float32),
+        ],
+        input_output_aliases=aliases,
+        compiler_params=pltpu.CompilerParams(vmem_limit_bytes=VMEM_LIMIT),
+    )(*parts, flip, mix, inverse, *(before or ()))
+
+
+def local_rows(raw_frames, dark_frame, flat_field, seeing, anchors, taper):
+    tile = lax.axis_index("tile")
+    segment = lax.axis_index("segment")
+    chip = tile // 2
+    core = tile % 2
+    n_sub = seeing.shape[1]
+    width = raw_frames.shape[2]
+    n_groups = width // GROUP
+    frame = raw_frames[0]
+
+    def along(step):
+        return [(2 * z + k, 2 * (z + step) + k) for z in range(4) for k in range(2) if 0 <= z + step < 4]
+
+    def right(x):
+        return lax.ppermute(x, "tile", along(1))
+
+    def left(x):
+        return lax.ppermute(x, "tile", along(-1))
+
+    def swap(x):
+        return lax.ppermute(x, "tile", [(t, t ^ 1) for t in range(8)])
+
+    own_rows = lax.dynamic_slice_in_dim(frame, 256 * chip, 512, 0)
+    cut = [slice(GROUP * g, GROUP * g + GROUP) for g in range(n_groups)]
+
+    gathered = []
+    gate_r = gate_l = None
+    for g in range(n_groups):
+        send_r = frame[768:1280, cut[g]]
+        send_l = frame[0:512, cut[g]]
+        if gate_r is not None:
+            send_r, gate_r = lax.optimization_barrier((send_r, gate_r))
+            send_l, gate_l = lax.optimization_barrier((send_l, gate_l))
+        r1 = right(send_r)
+        l1 = left(send_l)
+        gate_r, gate_l = r1, l1
+        r2 = right(jnp.where(chip == 0, frame[256:768, cut[g]], r1))
+        l2 = left(jnp.where(chip == 3, frame[512:1024, cut[g]], l1))
+        middle = frame[512:768, cut[g]]
+        r3 = right(jnp.where(chip == 1, jnp.concatenate([middle, r2[256:]], 0), r2))
+        l3 = left(jnp.where(chip == 2, jnp.concatenate([middle, l2[:256]], 0), l2))
+        own = own_rows[:, cut[g]]
+
+        def pick(a, b, c, d):
+            return jnp.where(chip == 0, a, jnp.where(chip == 1, b, jnp.where(chip == 2, c, d)))
+
+        def cat(a, b):
+            return jnp.concatenate([a, b], 0)
+
+        stack = jnp.stack(
+            [
+                pick(own, r2, cat(r3[256:], r2[:256]), r3),
+                pick(l1, own, cat(r3[:256], r1[:256]), r2),
+                pick(l2, cat(l1[256:], l3[:256]), own, r1),
+                pick(l3, cat(l2[256:], l3[256:]), l2, own),
+            ]
+        )
+        upper = stack[:, :REGION]
+        lower = stack[:, 128 : 128 + REGION]
+        keep = jnp.where(core == 0, upper, lower)
+        give = jnp.where(core == 0, lower, upper)
+        gathered.append((keep, swap(give)))
+
+    first_row = 128 * tile
+    dark = lax.dynamic_slice_in_dim(dark_frame, first_row, REGION, 0).astype(jnp.float32)
+    rate = 1.0 / lax.dynamic_slice_in_dim(flat_field, first_row, REGION, 0).astype(jnp.float32)
+    mine = lax.dynamic_slice_in_dim(anchors, n_sub * tile, n_sub, 0)
+    widths = lax.dynamic_slice_in_dim(taper, n_sub * tile, n_sub, 0)
+    top = mine[:, 0] - first_row
+    side = mine[:, 1] - 128 * jnp.arange(n_sub, dtype=jnp.int32)
+    ramp = shifted_ramps(widths, jnp.zeros_like(side), S)[:, :, None] * shifted_ramps(
+        widths, side, REGION
+    )[:, None, :]
+    cosine, sine = dft_tables(S)
+    wave = jnp.concatenate([cosine, -sine], axis=1).astype(jnp.float32)
+    wave = jnp.roll(jnp.concatenate([wave, wave], axis=0), 128, axis=0)
+    wave = wave.reshape(2 * S, 4, 128).transpose(1, 0, 2)
+    table = jnp.concatenate([cosine[:HALF], sine[:HALF]], axis=0)
+    inverse = 1.0 / jnp.sum(seeing, axis=0)
+    inverse = jnp.broadcast_to(inverse[:, None, None], (n_sub, 1, S))
+    row = jnp.arange(S, dtype=jnp.int32)
+    mirrored = segment >= 2
+    turn = jnp.stack([(S - row) % S, S - 1 - row])
+    turn = jnp.where(mirrored, turn, row[None, :])
+    flip = (turn[:, None, :] == row[None, :, None]).astype(jnp.bfloat16)
+    order = jnp.where(mirrored, 63 - row[:64], row[:64])
+    mix = (row[None, :] % 64 == order[:, None]).astype(jnp.bfloat16)
+
+    result = None
+    for p in range(n_groups - 1):
+        scal = jnp.concatenate(
+            [
+                jnp.stack([segment, 8 * segment, core, jnp.int32(2 * p)]),
+                jnp.stack([top[2 * p], side[2 * p], top[2 * p + 1], side[2 * p + 1]]),
+            ]
+        ).astype(jnp.int32)
+        own = (gathered[p][0], gathered[p + 1][0])
+        far = (gathered[p][1], gathered[p + 1][1])
+        partial = spectra(p, scal, seeing, own, far, dark, rate, ramp, wave, table)
+        parts = [partial[:1]]
+        for m in range(1, 4):
+            parts.append(lax.ppermute(partial[m : m + 1], "segment", [(s, s ^ m) for s in range(4)]))
+        result = finish(p, parts, flip, mix, inverse, result, n_sub)
+    return tuple(result)
+
+
 def solution(mesh):
     placed = (P(("segment", "tile"), None, None), P(), P(), P(None, "tile"), P(), P())
+    by_rows = mesh.shape["tile"] == 8 and mesh.shape["segment"] == 4
     return jax.shard_map(
-        local,
+        local_rows if by_rows else local_any,
         mesh=mesh,
         in_specs=placed,
         out_specs=(P("tile", "segment", None), P("tile", None, "segment", None)),

time: 752 us -> 278 us (0.37)
  local copies, waits for them, and re-layouts: 309 us -> 41.7 us
  waiting for transfers between devices: 251 us -> 31.3 us
  starting transfers between devices: 6.4 us -> 95 us
  other arithmetic: 109 us -> 35 us
  Pallas kernels: 0 us -> 71.1 us
  matrix products: 56.3 us -> 0 us
  between operations: 14.1 us -> 1.7 us
    gather x192 -> x0, local copies, waits for them, and re-layouts: 242 us -> none
    all_to_all x1 -> x0, waiting for transfers between devices: 182 us -> none  [local(): lax.all_to_all(sub, 'tile', split_axis=1, concat_axis=0, tiled=True)]
    ppermute x0 -> x47, starting transfers between devices: none -> 95 us  [the longest x15 60.7 us: right(): return lax.ppermute(x, 'tile', along(1))]
    pallas_call x0 -> x8, Pallas kernels: none -> 71.1 us  [the longest x4 53.2 us: spectra(): pl.pallas_call(spectra_kernel, name='spectra', grid_spec=pltpu.PrefetchSc...]
    reduce_scatter x2 -> x0, waiting for transfers between devices: 68.9 us -> none  [the longest x1 54 us: local(): lax.psum_scatter(cross_sum.astype(jnp.bfloat16), 'segment', scatter_dimen...]
    dot_general x3 -> x0, matrix products: 56.3 us -> none  [the longest x1 22.3 us: second_pass(): jnp.einsum('ux,fsxk->fsuk', sine, half, preferred_element_type=jnp.float32)]
    reduce_sum x3 -> x1, other arithmetic: 46.9 us -> 0.12 us  [local_rows(): inverse = 1.0 / jnp.sum(seeing, axis=0)]
    add x1 -> x0, other arithmetic: 34 us -> none  [second_pass(): real_part = with_cos[..., :size] + with_sin[..., size:]]
  transfers between devices with their start and end apart: 3 -> 47, of which waited for: 3 -> 17; matrix products, arithmetic and copies ran while one was open for 2% -> 25% of each run, Pallas kernels for 0% -> 24%
where the time goes in v1:
time: 278 us; the launch traced here: 276 us
  starting transfers between devices  95 us (34%)
  Pallas kernels  71.1 us (26%)
  local copies, waits for them, and re-layouts  41.7 us (15%)
  other arithmetic  35 us (13%)
  waiting for transfers between devices  31.3 us (11%)
    ppermute x15, starting transfers between devices, right(): return lax.ppermute(x, 'tile', along(1))  60.7 us
    pallas_call x4, Pallas kernels, spectra(): pl.pallas_call(spectra_kernel, name='spectra', grid_spec=pltpu.PrefetchSc...  53.2 us
    ppermute x15, starting transfers between devices, left(): return lax.ppermute(x, 'tile', along(-1))  19.4 us
    ppermute x15, waiting for transfers between devices, left(): return lax.ppermute(x, 'tile', along(-1))  18.8 us
    pallas_call x4, Pallas kernels, finish(): pl.pallas_call(finish_kernel, name='finish', grid=(1,), in_specs=specs, o...  17.9 us
    ppermute x12, starting transfers between devices, local_rows(): lax.ppermute(partial[m:m + 1], 'segment', [(s, s ^ m) for s in range(4)])  14.4 us
    concatenate x4, local copies, waits for them, and re-layouts, local_rows(): jnp.concatenate([jnp.stack([segment, 8 * segment, core, jnp.int32(2 * p)]...  12.7 us
    ppermute x15, waiting for transfers between devices, right(): return lax.ppermute(x, 'tile', along(1))  10.6 us
  transfers between devices with their start and end apart: 47, of which 17 were waited for; matrix products, arithmetic and copies ran while one was open for 25% of the time, Pallas kernels for 24%

profile of v1, /device:TPU:0, one launch (start us, length us, event | category | flops | bytes accessed | tf_op | source)
XLA Modules:
  0.0 275.8 jit_solution(12885124531342664911)
XLA Ops:
  5.0 5.6 %collective-permute-start = (bf16[512,256]{1,0:T(8,128)(2,1)}, bf16[512,256]{1,0:T(8,128)(2,1)S(1)}, u32[]{:S(2)}, u32[]{:S(2)}) collective-permute-start(bf16[512,256]{1,0:T(8,128)(2,1)} %get-tuple-element.51), channel_id=1, source_target_pairs={{0,2},{1,3},{2,4},{3,5},{4,6},{5,7},{8,10},{9,11},{10,12},{11,13},... | collective-permute-start | bytes 786440 | tf_op jit(solution)/shard_map/ppermute | solution.py:324
  26.4 7.0 %collective-permute-done.7 = bf16[512,256]{1,0:T(8,128)(2,1)} collective-permute-done((bf16[512,256]{1,0:T(8,128)(2,1)}, bf16[512,256]{1,0:T(8,128)(2,1)}, u32[]{:S(2)}, u32[]{:S(2)}) %collective-permute-start.7) | collective-permute-done | bytes 262176 | tf_op jit(solution)/shard_map/ppermute | solution.py:327
  37.1 5.5 %collective-permute-start.1 = (bf16[512,256]{1,0:T(8,128)(2,1)}, bf16[512,256]{1,0:T(8,128)(2,1)}, u32[]{:S(2)}, u32[]{:S(2)}) collective-permute-start(bf16[512,256]{1,0:T(8,128)(2,1)} %get-tuple-element.16), channel_id=1, source_target_pairs={{0,2},{1,3},{2,4},{3,5},{4,6},{5,7},{8,10},{9,11},{10,12},{11,13},... | collective-permute-start | bytes 786440 | tf_op jit(solution)/shard_map/ppermute | solution.py:324
  46.6 4.4 %collective-permute-start.2 = (bf16[512,256]{1,0:T(8,128)(2,1)}, bf16[512,256]{1,0:T(8,128)(2,1)S(1)}, u32[]{:S(2)}, u32[]{:S(2)}) collective-permute-start(bf16[512,256]{1,0:T(8,128)(2,1)} %get-tuple-element.17), channel_id=1, source_target_pairs={{0,2},{1,3},{2,4},{3,5},{4,6},{5,7},{8,10},{9,11},{10,12},{11,13},... | collective-permute-start | bytes 786440 | tf_op jit(solution)/shard_map/ppermute | solution.py:324
  55.2 5.1 %collective-permute-start.3 = (bf16[512,256]{1,0:T(8,128)(2,1)}, bf16[512,256]{1,0:T(8,128)(2,1)}, u32[]{:S(2)}, u32[]{:S(2)}) collective-permute-start(bf16[512,256]{1,0:T(8,128)(2,1)} %get-tuple-element.18), channel_id=1, source_target_pairs={{0,2},{1,3},{2,4},{3,5},{4,6},{5,7},{8,10},{9,11},{10,12},{11,13},... | collective-permute-start | bytes 786440 | tf_op jit(solution)/shard_map/ppermute | solution.py:324
  63.1 3.7 %collective-permute-start.39 = (bf16[512,256]{1,0:T(8,128)(2,1)}, bf16[512,256]{1,0:T(8,128)(2,1)S(1)}, u32[]{:S(2)}, u32[]{:S(2)}) collective-permute-start(bf16[512,256]{1,0:T(8,128)(2,1)} %get-tuple-element.30), channel_id=1, source_target_pairs={{0,2},{1,3},{2,4},{3,5},{4,6},{5,7},{8,10},{9,11},{10,12},{11,13},... | collective-permute-start | bytes 786440 | tf_op jit(solution)/shard_map/ppermute | solution.py:324
  80.6 3.3 %concatenate.119.scal = s32[8]{0:T(128)} concatenate(s32[1]{0:T(128)} %bitcast, s32[1]{0:T(128)} %bitcast.1, s32[1]{0:T(128)} %bitcast.2, s32[1]{0:T(128)} %constant.100.clone.1, s32[1]{0:T(128)} %bitcast.3, s32[1]{0:T(128)} %get-tuple-element.160, s32[1]{0:T(128)} %bitcast.5, s32[1]{0:T(128)} %get-tuple-element.159), dimensions={0} | concatenate | bytes 64 | tf_op jit(solution)/shard_map/concatenate | solution.py:400
  87.8 4.6 %collective-permute-start.12 = (bf16[512,256]{1,0:T(8,128)(2,1)S(1)}, bf16[512,256]{1,0:T(8,128)(2,1)S(1)}, u32[]{:S(2)}, u32[]{:S(2)}) collective-permute-start(bf16[512,256]{1,0:T(8,128)(2,1)S(1)} %copy-done.39), channel_id=1, source_target_pairs={{0,2},{1,3},{2,4},{3,5},{4,6},{5,7},{8,10},{9,11},{10,12},{11,13},... | collective-permute-start | bytes 786440 | tf_op jit(solution)/shard_map/ppermute | solution.py:324
  93.7 4.6 %collective-permute-start.31 = (bf16[512,256]{1,0:T(8,128)(2,1)S(1)}, bf16[512,256]{1,0:T(8,128)(2,1)S(1)}, u32[]{:S(2)}, u32[]{:S(2)}) collective-permute-start(bf16[512,256]{1,0:T(8,128)(2,1)S(1)} %copy-done.44), channel_id=1, source_target_pairs={{0,2},{1,3},{2,4},{3,5},{4,6},{5,7},{8,10},{9,11},{10,12},{11,13},... | collective-permute-start | bytes 786440 | tf_op jit(solution)/shard_map/ppermute | solution.py:324
  99.8 4.6 %collective-permute-start.23 = (bf16[512,256]{1,0:T(8,128)(2,1)S(1)}, bf16[512,256]{1,0:T(8,128)(2,1)S(1)}, u32[]{:S(2)}, u32[]{:S(2)}) collective-permute-start(bf16[512,256]{1,0:T(8,128)(2,1)S(1)} %copy-done.42), channel_id=1, source_target_pairs={{0,2},{1,3},{2,4},{3,5},{4,6},{5,7},{8,10},{9,11},{10,12},{11,13},... | collective-permute-start | bytes 786440 | tf_op jit(solution)/shard_map/ppermute | solution.py:324
  109.4 4.9 %collective-permute-start.40 = (bf16[512,256]{1,0:T(8,128)(2,1)S(1)}, bf16[512,256]{1,0:T(8,128)(2,1)S(1)}, u32[]{:S(2)}, u32[]{:S(2)}) collective-permute-start(bf16[512,256]{1,0:T(8,128)(2,1)S(1)} %get-tuple-element.143), channel_id=1, source_target_pairs={{0,2},{1,3},{2,4},{3,5},{4,6},{5,7},{8,10},{9,11},{10,12},{11,13},... | collective-permute-start | bytes 786440 | tf_op jit(solution)/shard_map/ppermute | solution.py:324
  116.1 4.1 %collective-permute-done.10 = bf16[512,256]{1,0:T(8,128)(2,1)S(1)} collective-permute-done((bf16[512,256]{1,0:T(8,128)(2,1)S(1)}, bf16[512,256]{1,0:T(8,128)(2,1)S(1)}, u32[]{:S(2)}, u32[]{:S(2)}) %collective-permute-start.10) | collective-permute-done | bytes 262176 | tf_op jit(solution)/shard_map/ppermute | solution.py:327
  129.1 4.4 %collective-permute-start.24 = (bf16[512,256]{1,0:T(8,128)(2,1)S(1)}, bf16[512,256]{1,0:T(8,128)(2,1)S(1)}, u32[]{:S(2)}, u32[]{:S(2)}) collective-permute-start(bf16[512,256]{1,0:T(8,128)(2,1)S(1)} %get-tuple-element.147), channel_id=1, source_target_pairs={{0,2},{1,3},{2,4},{3,5},{4,6},{5,7},{8,10},{9,11},{10,12},{11,13},... | collective-permute-start | bytes 786440 | tf_op jit(solution)/shard_map/ppermute | solution.py:324
  137.5 3.5 %collective-permute-start.13 = (bf16[512,256]{1,0:T(8,128)(2,1)S(1)}, bf16[512,256]{1,0:T(8,128)(2,1)S(1)}, u32[]{:S(2)}, u32[]{:S(2)}) collective-permute-start(bf16[512,256]{1,0:T(8,128)(2,1)S(1)} %get-tuple-element.44), channel_id=1, source_target_pairs={{0,2},{1,3},{2,4},{3,5},{4,6},{5,7},{8,10},{9,11},{10,12},{11,13},... | collective-permute-start | bytes 786440 | tf_op jit(solution)/shard_map/ppermute | solution.py:324
  157.6 4.5 %collective-permute-done.5 = bf16[512,256]{1,0:T(8,128)(2,1)S(1)} collective-permute-done((bf16[512,256]{1,0:T(8,128)(2,1)S(1)}, bf16[512,256]{1,0:T(8,128)(2,1)S(1)}, u32[]{:S(2)}, u32[]{:S(2)}) %collective-permute-start.5) | collective-permute-done | bytes 262176 | tf_op jit(solution)/shard_map/ppermute | solution.py:324
  167.6 4.6 %collective-permute-done.17 = bf16[512,256]{1,0:T(8,128)(2,1)S(1)} collective-permute-done((bf16[512,256]{1,0:T(8,128)(2,1)S(1)}, bf16[512,256]{1,0:T(8,128)(2,1)S(1)}, u32[]{:S(2)}, u32[]{:S(2)}) %collective-permute-start.17) | collective-permute-done | bytes 262176 | tf_op jit(solution)/shard_map/ppermute | solution.py:327
  175.7 13.3 %spectra.7 = bf16[4,2,5,64,256]{4,3,2,1,0:T(8,128)(2,1)} custom-call(s32[8]{0:T(128)} %concatenate.150.scal, f32[32,8]{1,0:T(8,128)} %copy.15.wgt, bf16[4,384,256]{2,1,0:T(8,128)(2,1)} %get-tuple-element.92.own0, bf16[4,384,256]{2,1,0:T(8,128)(2,1)} %get-tuple-element.94.own0.own1, bf16[4,384,256]{2,1,0:T(8,128)(2,1)} %copy-done.24, ...), custom_call_target="tpu_custom_call" | custom-call | tf_op jit(solution)/shard_map/spectra/pallas_call | solution.py:229
  195.1 13.3 %spectra.6 = bf16[4,2,5,64,256]{4,3,2,1,0:T(8,128)(2,1)} custom-call(s32[8]{0:T(128)} %concatenate.143.scal, f32[32,8]{1,0:T(8,128)} %copy.15.wgt, bf16[4,384,256]{2,1,0:T(8,128)(2,1)} %get-tuple-element.94.own0.own1, bf16[4,384,256]{2,1,0:T(8,128)(2,1)} %get-tuple-element.96.own0.own1, bf16[4,384,256]{2,1,0:T(8,128)(2,1)} %copy-done.5, ...), custom_call_target="tpu_custom_call" | custom-call | tf_op jit(solution)/shard_map/spectra/pallas_call | solution.py:229
  213.7 13.3 %spectra.5 = bf16[4,2,5,64,256]{4,3,2,1,0:T(8,128)(2,1)} custom-call(s32[8]{0:T(128)} %concatenate.136.scal, f32[32,8]{1,0:T(8,128)} %copy.15.wgt, bf16[4,384,256]{2,1,0:T(8,128)(2,1)} %get-tuple-element.96.own0.own1, bf16[4,384,256]{2,1,0:T(8,128)(2,1)} %get-tuple-element.100.own0.own1, bf16[4,384,256]{2,1,0:T(8,128)(2,1)} %copy-done.6, ...), custom_call_target="tpu_custom_call" | custom-call | tf_op jit(solution)/shard_map/spectra/pallas_call | solution.py:229
  232.7 13.3 %spectra.4 = bf16[4,2,5,64,256]{4,3,2,1,0:T(8,128)(2,1)} custom-call(s32[8]{0:T(128)} %concatenate.119.scal, f32[32,8]{1,0:T(8,128)} %copy.15.wgt, bf16[4,384,256]{2,1,0:T(8,128)(2,1)} %get-tuple-element.100.own0.own1, bf16[4,384,256]{2,1,0:T(8,128)(2,1)} %get-tuple-element.98.own1, bf16[4,384,256]{2,1,0:T(8,128)(2,1)} %copy-done.7, ...), custom_call_target="tpu_custom_call" | custom-call | tf_op jit(solution)/shard_map/spectra/pallas_call | solution.py:229
  254.5 4.5 %finish.4 = (f32[8,64,256]{2,1,0:T(8,128)}, f32[8,4,64,256]{3,2,1,0:T(8,128)}) custom-call(bf16[1,2,5,64,256]{4,3,2,1,0:T(8,128)(2,1)} %get-tuple-element.78.mine, bf16[1,2,5,64,256]{4,3,2,1,0:T(8,128)(2,1)} %collective-permute-done.44.got1, bf16[1,2,5,64,256]{4,3,2,1,0:T(8,128)(2,1)} %collective-permute-done.45.got2, ...), custom_call_target="tpu_custom_call" | custom-call | tf_op jit(solution)/shard_map/finish/pallas_call | solution.py:292
  259.0 4.5 %finish.5 = (f32[8,64,256]{2,1,0:T(8,128)}, f32[8,4,64,256]{3,2,1,0:T(8,128)}) custom-call(bf16[1,2,5,64,256]{4,3,2,1,0:T(8,128)(2,1)} %get-tuple-element.82.mine, bf16[1,2,5,64,256]{4,3,2,1,0:T(8,128)(2,1)} %copy-done.33, bf16[1,2,5,64,256]{4,3,2,1,0:T(8,128)(2,1)} %copy-done.32, ...), custom_call_target="tpu_custom_call", output_to_operand_aliasing={{0}: (7, {}), {1}: (8, {})} | custom-call | tf_op jit(solution)/shard_map/finish/pallas_call | solution.py:292
  265.1 4.5 %finish.6 = (f32[8,64,256]{2,1,0:T(8,128)}, f32[8,4,64,256]{3,2,1,0:T(8,128)}) custom-call(bf16[1,2,5,64,256]{4,3,2,1,0:T(8,128)(2,1)} %get-tuple-element.86.mine, bf16[1,2,5,64,256]{4,3,2,1,0:T(8,128)(2,1)} %copy-done.37, bf16[1,2,5,64,256]{4,3,2,1,0:T(8,128)(2,1)} %copy-done.35, ...), custom_call_target="tpu_custom_call", output_to_operand_aliasing={{0}: (7, {}), {1}: (8, {})} | custom-call | tf_op jit(solution)/shard_map/finish/pallas_call | solution.py:292
  271.4 4.5 %finish.7 = (f32[8,64,256]{2,1,0:T(8,128)}, f32[8,4,64,256]{3,2,1,0:T(8,128)}) custom-call(bf16[1,2,5,64,256]{4,3,2,1,0:T(8,128)(2,1)} %get-tuple-element.90.mine, bf16[1,2,5,64,256]{4,3,2,1,0:T(8,128)(2,1)} %copy-done.38, bf16[1,2,5,64,256]{4,3,2,1,0:T(8,128)(2,1)} %copy-done.36, ...), custom_call_target="tpu_custom_call", output_to_operand_aliasing={{0}: (7, {}), {1}: (8, {})} | custom-call | tf_op jit(solution)/shard_map/finish/pallas_call | solution.py:292
  (285 shorter events, 128.7 us)
Async XLA Ops:
  3.7 19.7 %collective-permute-start.6 = (bf16[512,256]{1,0:T(8,128)(2,1)}, bf16[512,256]{1,0:T(8,128)(2,1)}, u32[]{:S(2)}, u32[]{:S(2)}) collective-permute-start(bf16[512,256]{1,0:T(8,128)(2,1)} %get-tuple-element.47), channel_id=1, source_target_pairs={{2,0},{3,1},{4,2},{5,3},{6,4},{7,5},{10,8},{11,9},{12,10},{13,11},... | collective-permute-start | bytes 786440 | tf_op jit(solution)/shard_map/ppermute | solution.py:327
  5.0 32.1 %collective-permute-start = (bf16[512,256]{1,0:T(8,128)(2,1)}, bf16[512,256]{1,0:T(8,128)(2,1)S(1)}, u32[]{:S(2)}, u32[]{:S(2)}) collective-permute-start(bf16[512,256]{1,0:T(8,128)(2,1)} %get-tuple-element.51), channel_id=1, source_target_pairs={{0,2},{1,3},{2,4},{3,5},{4,6},{5,7},{8,10},{9,11},{10,12},{11,13},... | collective-permute-start | bytes 786440 | tf_op jit(solution)/shard_map/ppermute | solution.py:324
  55.2 31.7 %collective-permute-start.3 = (bf16[512,256]{1,0:T(8,128)(2,1)}, bf16[512,256]{1,0:T(8,128)(2,1)}, u32[]{:S(2)}, u32[]{:S(2)}) collective-permute-start(bf16[512,256]{1,0:T(8,128)(2,1)} %get-tuple-element.18), channel_id=1, source_target_pairs={{0,2},{1,3},{2,4},{3,5},{4,6},{5,7},{8,10},{9,11},{10,12},{11,13},... | collective-permute-start | bytes 786440 | tf_op jit(solution)/shard_map/ppermute | solution.py:324
  63.1 35.2 %collective-permute-start.39 = (bf16[512,256]{1,0:T(8,128)(2,1)}, bf16[512,256]{1,0:T(8,128)(2,1)S(1)}, u32[]{:S(2)}, u32[]{:S(2)}) collective-permute-start(bf16[512,256]{1,0:T(8,128)(2,1)} %get-tuple-element.30), channel_id=1, source_target_pairs={{0,2},{1,3},{2,4},{3,5},{4,6},{5,7},{8,10},{9,11},{10,12},{11,13},... | collective-permute-start | bytes 786440 | tf_op jit(solution)/shard_map/ppermute | solution.py:324
  68.6 31.2 %collective-permute-start.41 = (bf16[512,256]{1,0:T(8,128)(2,1)}, bf16[512,256]{1,0:T(8,128)(2,1)}, u32[]{:S(2)}, u32[]{:S(2)}) collective-permute-start(bf16[512,256]{1,0:T(8,128)(2,1)} %get-tuple-element.31), channel_id=1, source_target_pairs={{2,0},{3,1},{4,2},{5,3},{6,4},{7,5},{10,8},{11,9},{12,10},{13,11},... | collective-permute-start | bytes 786440 | tf_op jit(solution)/shard_map/ppermute | solution.py:327
  87.8 37.2 %collective-permute-start.12 = (bf16[512,256]{1,0:T(8,128)(2,1)S(1)}, bf16[512,256]{1,0:T(8,128)(2,1)S(1)}, u32[]{:S(2)}, u32[]{:S(2)}) collective-permute-start(bf16[512,256]{1,0:T(8,128)(2,1)S(1)} %copy-done.39), channel_id=1, source_target_pairs={{0,2},{1,3},{2,4},{3,5},{4,6},{5,7},{8,10},{9,11},{10,12},{11,13},... | collective-permute-start | bytes 786440 | tf_op jit(solution)/shard_map/ppermute | solution.py:324
  109.4 34.1 %collective-permute-start.40 = (bf16[512,256]{1,0:T(8,128)(2,1)S(1)}, bf16[512,256]{1,0:T(8,128)(2,1)S(1)}, u32[]{:S(2)}, u32[]{:S(2)}) collective-permute-start(bf16[512,256]{1,0:T(8,128)(2,1)S(1)} %get-tuple-element.143), channel_id=1, source_target_pairs={{0,2},{1,3},{2,4},{3,5},{4,6},{5,7},{8,10},{9,11},{10,12},{11,13},... | collective-permute-start | bytes 786440 | tf_op jit(solution)/shard_map/ppermute | solution.py:324
  114.6 33.1 %collective-permute-start.42 = (bf16[512,256]{1,0:T(8,128)(2,1)S(1)}, bf16[512,256]{1,0:T(8,128)(2,1)S(1)}, u32[]{:S(2)}, u32[]{:S(2)}) collective-permute-start(bf16[512,256]{1,0:T(8,128)(2,1)S(1)} %get-tuple-element.144), channel_id=1, source_target_pairs={{2,0},{3,1},{4,2},{5,3},{6,4},{7,5},{10,8},{11,9},{12,10},{13,11},... | collective-permute-start | bytes 786440 | tf_op jit(solution)/shard_map/ppermute | solution.py:327
  129.1 22.2 %collective-permute-start.24 = (bf16[512,256]{1,0:T(8,128)(2,1)S(1)}, bf16[512,256]{1,0:T(8,128)(2,1)S(1)}, u32[]{:S(2)}, u32[]{:S(2)}) collective-permute-start(bf16[512,256]{1,0:T(8,128)(2,1)S(1)} %get-tuple-element.147), channel_id=1, source_target_pairs={{0,2},{1,3},{2,4},{3,5},{4,6},{5,7},{8,10},{9,11},{10,12},{11,13},... | collective-permute-start | bytes 786440 | tf_op jit(solution)/shard_map/ppermute | solution.py:324
  151.3 22.6 %collective-permute-start.43 = (bf16[4,384,256]{2,1,0:T(8,128)(2,1)S(1)}, bf16[4,384,256]{2,1,0:T(8,128)(2,1)S(1)}, u32[]{:S(2)}, u32[]{:S(2)}) collective-permute-start(bf16[4,384,256]{2,1,0:T(8,128)(2,1)S(1)} %get-tuple-element.91), channel_id=1, source_target_pairs={{0,1},{1,0},{2,3},{3,2},{4,5},{5,4},{6,7},{7,6},{8,9},{9,8},{10,11... | collective-permute-start | bytes 2359304 | tf_op jit(solution)/shard_map/ppermute | solution.py:330
  151.3 22.6 %collective-permute-start.35 = (bf16[4,384,256]{2,1,0:T(8,128)(2,1)S(1)}, bf16[4,384,256]{2,1,0:T(8,128)(2,1)S(1)}, u32[]{:S(2)}, u32[]{:S(2)}) collective-permute-start(bf16[4,384,256]{2,1,0:T(8,128)(2,1)S(1)} %get-tuple-element.93), channel_id=1, source_target_pairs={{0,1},{1,0},{2,3},{3,2},{4,5},{5,4},{6,7},{7,6},{8,9},{9,8},{10,11... | collective-permute-start | bytes 2359304 | tf_op jit(solution)/shard_map/ppermute | solution.py:330
  153.8 40.5 %collective-permute-start.27 = (bf16[4,384,256]{2,1,0:T(8,128)(2,1)S(1)}, bf16[4,384,256]{2,1,0:T(8,128)(2,1)S(1)}, u32[]{:S(2)}, u32[]{:S(2)}) collective-permute-start(bf16[4,384,256]{2,1,0:T(8,128)(2,1)S(1)} %get-tuple-element.95), channel_id=1, source_target_pairs={{0,1},{1,0},{2,3},{3,2},{4,5},{5,4},{6,7},{7,6},{8,9},{9,8},{10,11... | collective-permute-start | bytes 2359304 | tf_op jit(solution)/shard_map/ppermute | solution.py:330
  167.3 44.0 %collective-permute-start.18 = (bf16[4,384,256]{2,1,0:T(8,128)(2,1)S(1)}, bf16[4,384,256]{2,1,0:T(8,128)(2,1)S(1)}, u32[]{:S(2)}, u32[]{:S(2)}) collective-permute-start(bf16[4,384,256]{2,1,0:T(8,128)(2,1)S(1)} %get-tuple-element.99), channel_id=1, source_target_pairs={{0,1},{1,0},{2,3},{3,2},{4,5},{5,4},{6,7},{7,6},{8,9},{9,8},{10,11... | collective-permute-start | bytes 2359304 | tf_op jit(solution)/shard_map/ppermute | solution.py:330
  173.9 56.7 %collective-permute-start.19 = (bf16[4,384,256]{2,1,0:T(8,128)(2,1)}, bf16[4,384,256]{2,1,0:T(8,128)(2,1)}, u32[]{:S(2)}, u32[]{:S(2)}) collective-permute-start(bf16[4,384,256]{2,1,0:T(8,128)(2,1)} %get-tuple-element.97), channel_id=1, source_target_pairs={{0,1},{1,0},{2,3},{3,2},{4,5},{5,4},{6,7},{7,6},{8,9},{9,8},{10,11... | collective-permute-start | bytes 2359304 | tf_op jit(solution)/shard_map/ppermute | solution.py:330
  191.3 37.9 %collective-permute-start.46 = (bf16[1,2,5,64,256]{4,3,2,1,0:T(8,128)(2,1)}, bf16[1,2,5,64,256]{4,3,2,1,0:T(8,128)(2,1)}, u32[]{:S(2)}, u32[]{:S(2)}) collective-permute-start(bf16[1,2,5,64,256]{4,3,2,1,0:T(8,128)(2,1)} %get-tuple-element.75), channel_id=1, source_target_pairs={{0,24},{8,16},{16,8},{24,0},{1,25},{9,17},{17,9},{25,1},{2,26},{10... | collective-permute-start | bytes 983048 | tf_op jit(solution)/shard_map/ppermute | solution.py:411
  193.7 35.9 %collective-permute-start.45 = (bf16[1,2,5,64,256]{4,3,2,1,0:T(8,128)(2,1)S(1)}, bf16[1,2,5,64,256]{4,3,2,1,0:T(8,128)(2,1)}, u32[]{:S(2)}, u32[]{:S(2)}) collective-permute-start(bf16[1,2,5,64,256]{4,3,2,1,0:T(8,128)(2,1)S(1)} %get-tuple-element.76), channel_id=1, source_target_pairs={{0,16},{8,24},{16,0},{24,8},{1,17},{9,25},{17,1},{25,9},{2,18},{10... | collective-permute-start | bytes 983048 | tf_op jit(solution)/shard_map/ppermute | solution.py:411
  210.7 37.4 %collective-permute-start.44 = (bf16[1,2,5,64,256]{4,3,2,1,0:T(8,128)(2,1)S(1)}, bf16[1,2,5,64,256]{4,3,2,1,0:T(8,128)(2,1)}, u32[]{:S(2)}, u32[]{:S(2)}) collective-permute-start(bf16[1,2,5,64,256]{4,3,2,1,0:T(8,128)(2,1)S(1)} %get-tuple-element.77), channel_id=1, source_target_pairs={{0,8},{8,0},{16,24},{24,16},{1,9},{9,1},{17,25},{25,17},{2,10},{10... | collective-permute-start | bytes 983048 | tf_op jit(solution)/shard_map/ppermute | solution.py:411
  211.3 37.4 %collective-permute-start.38 = (bf16[1,2,5,64,256]{4,3,2,1,0:T(8,128)(2,1)}, bf16[1,2,5,64,256]{4,3,2,1,0:T(8,128)(2,1)S(1)}, u32[]{:S(2)}, u32[]{:S(2)}) collective-permute-start(bf16[1,2,5,64,256]{4,3,2,1,0:T(8,128)(2,1)} %get-tuple-element.79), channel_id=1, source_target_pairs={{0,24},{8,16},{16,8},{24,0},{1,25},{9,17},{17,9},{25,1},{2,26},{10... | collective-permute-start | bytes 983048 | tf_op jit(solution)/shard_map/ppermute | solution.py:411
  229.2 20.4 %collective-permute-start.37 = (bf16[1,2,5,64,256]{4,3,2,1,0:T(8,128)(2,1)}, bf16[1,2,5,64,256]{4,3,2,1,0:T(8,128)(2,1)S(1)}, u32[]{:S(2)}, u32[]{:S(2)}) collective-permute-start(bf16[1,2,5,64,256]{4,3,2,1,0:T(8,128)(2,1)} %get-tuple-element.80), channel_id=1, source_target_pairs={{0,16},{8,24},{16,0},{24,8},{1,17},{9,25},{17,1},{25,9},{2,18},{10... | collective-permute-start | bytes 983048 | tf_op jit(solution)/shard_map/ppermute | solution.py:411
  229.7 22.0 %collective-permute-start.36 = (bf16[1,2,5,64,256]{4,3,2,1,0:T(8,128)(2,1)S(1)}, bf16[1,2,5,64,256]{4,3,2,1,0:T(8,128)(2,1)S(1)}, u32[]{:S(2)}, u32[]{:S(2)}) collective-permute-start(bf16[1,2,5,64,256]{4,3,2,1,0:T(8,128)(2,1)S(1)} %get-tuple-element.81), channel_id=1, source_target_pairs={{0,8},{8,0},{16,24},{24,16},{1,9},{9,1},{17,25},{25,17},{2,10},{10... | collective-permute-start | bytes 983048 | tf_op jit(solution)/shard_map/ppermute | solution.py:411
  230.6 21.5 %collective-permute-start.30 = (bf16[1,2,5,64,256]{4,3,2,1,0:T(8,128)(2,1)S(1)}, bf16[1,2,5,64,256]{4,3,2,1,0:T(8,128)(2,1)S(1)}, u32[]{:S(2)}, u32[]{:S(2)}) collective-permute-start(bf16[1,2,5,64,256]{4,3,2,1,0:T(8,128)(2,1)S(1)} %get-tuple-element.83), channel_id=1, source_target_pairs={{0,24},{8,16},{16,8},{24,0},{1,25},{9,17},{17,9},{25,1},{2,26},{10... | collective-permute-start | bytes 983048 | tf_op jit(solution)/shard_map/ppermute | solution.py:411
  249.6 20.0 %collective-permute-start.22 = (bf16[1,2,5,64,256]{4,3,2,1,0:T(8,128)(2,1)S(1)}, bf16[1,2,5,64,256]{4,3,2,1,0:T(8,128)(2,1)S(1)}, u32[]{:S(2)}, u32[]{:S(2)}) collective-permute-start(bf16[1,2,5,64,256]{4,3,2,1,0:T(8,128)(2,1)S(1)} %get-tuple-element.87), channel_id=1, source_target_pairs={{0,24},{8,16},{16,8},{24,0},{1,25},{9,17},{17,9},{25,1},{2,26},{10... | collective-permute-start | bytes 983048 | tf_op jit(solution)/shard_map/ppermute | solution.py:411
  251.6 18.7 %collective-permute-start.21 = (bf16[1,2,5,64,256]{4,3,2,1,0:T(8,128)(2,1)S(1)}, bf16[1,2,5,64,256]{4,3,2,1,0:T(8,128)(2,1)S(1)}, u32[]{:S(2)}, u32[]{:S(2)}) collective-permute-start(bf16[1,2,5,64,256]{4,3,2,1,0:T(8,128)(2,1)S(1)} %get-tuple-element.88), channel_id=1, source_target_pairs={{0,16},{8,24},{16,0},{24,8},{1,17},{9,25},{17,1},{25,9},{2,18},{10... | collective-permute-start | bytes 983048 | tf_op jit(solution)/shard_map/ppermute | solution.py:411
  252.1 18.5 %collective-permute-start.20 = (bf16[1,2,5,64,256]{4,3,2,1,0:T(8,128)(2,1)S(1)}, bf16[1,2,5,64,256]{4,3,2,1,0:T(8,128)(2,1)S(1)}, u32[]{:S(2)}, u32[]{:S(2)}) collective-permute-start(bf16[1,2,5,64,256]{4,3,2,1,0:T(8,128)(2,1)S(1)} %get-tuple-element.89), channel_id=1, source_target_pairs={{0,8},{8,0},{16,24},{24,16},{1,9},{9,1},{17,25},{25,17},{2,10},{10... | collective-permute-start | bytes 983048 | tf_op jit(solution)/shard_map/ppermute | solution.py:411
  (79 other events, 735.1 us)

commit v2 on v1

--- a/solution.py
+++ b/solution.py
@@ -1,3 +1,4 @@
+import functools
 import math
 
 import jax
@@ -8,7 +9,7 @@
 from jax.sharding import PartitionSpec as P
 
 S = 256
-GROUP = 256
+COLUMN_BLOCKS = (4, 3, 2, 1)
 REGION = 384
 HALF = 136
 VMEM_LIMIT = 60000 * 1024
@@ -130,19 +131,22 @@
     return jnp.where(inside, side(place) * side(S - 1 - place), 0.0)
 
 
-def spectra_kernel(
-    scal, wgt, own0, own1, far0, far1, dark0, dark1, rate0, rate1, ramp, wave, table, out,
-    cal, shifted, real, imag, sums,
-):
+def spectra_kernel(n_sub, first_sub, frames, tops, sides, spot, wgt, *refs):
+    slabs = n_sub + 2
+    raw = (refs[:slabs], refs[slabs : 2 * slabs])
+    darks = refs[2 * slabs : 3 * slabs]
+    rates = refs[3 * slabs : 4 * slabs]
+    ramp, wave, table = refs[4 * slabs : 4 * slabs + 3]
+    outs = refs[4 * slabs + 3 : 4 * slabs + 7]
+    cal, shifted, real, imag, sums = refs[4 * slabs + 7 :]
     step = pl.program_id(0)
-    pair = ramp.shape[0]
-    segment = scal[0]
+    segment = spot[0]
 
     @pl.when(step == 0)
     def _():
         sums[...] = jnp.zeros_like(sums)
-        for j in range(pair):
-            first = 128 - scal[4 + 2 * j + 1]
+        for j in range(n_sub):
+            first = 128 - sides[first_sub + j]
             for m in range(4):
                 shifted[j, :, 128 * m : 128 * m + 128] = wave[m, pl.ds(first, REGION), :].astype(
                     jnp.bfloat16
@@ -151,18 +155,14 @@
     lane = lax.broadcasted_iota(jnp.int32, (1, 128), 1)
     last_lane = lax.broadcasted_iota(jnp.int32, (8, 128), 1) == 127
     for near in range(2):
-        for m in range(4):
-            left = (own0, far0)[near] if m < 2 else (own1, far1)[near]
-            dark = dark0 if m < 2 else dark1
-            rate = rate0 if m < 2 else rate1
-            cols = slice(128 * (m % 2), 128 * (m % 2) + 128)
-            cal[near, m] = (left[0, :, cols].astype(jnp.float32) - dark[:, cols]) * rate[:, cols]
+        for c in range(slabs):
+            cal[near, c] = (raw[near][c][0].astype(jnp.float32) - darks[c][...]) * rates[c][...]
     for near in range(2):
-        frame = scal[1] + 2 * step + (scal[2] if near == 0 else 1 - scal[2])
-        for j in range(pair):
-            top = scal[4 + 2 * j]
-            left = scal[4 + 2 * j + 1]
-            weight = wgt[frame, scal[3] + j]
+        frame = frames[4 * near + step]
+        for j in range(n_sub):
+            top = tops[first_sub + j]
+            left = sides[first_sub + j]
+            weight = wgt[frame, first_sub + j]
             pieces = [cal[near, j + m, pl.ds(top, S), :] for m in range(3)]
             total = [jnp.sum(piece, axis=0, keepdims=True) for piece in pieces]
             total = (
@@ -208,65 +208,68 @@
 
     @pl.when(step == pl.num_programs(0) - 1)
     def _():
-        for target in range(4):
-            slot = jnp.bitwise_xor(segment, target)
-            for j in range(pair):
+        for slot in range(4):
+            target = jnp.bitwise_xor(segment, slot)
+            middle = (target == 1) | (target == 2)
+            shared = jnp.where(middle, 64, 0)
+            kept = shared + jnp.where(target >= 2, 1, 0)
+            for j in range(n_sub):
                 for plane in range(5):
-                    first = (0, 64, 64, 0)[target]
-                    if plane not in (1, 2):
-                        first = (0, 64, 65, 1)[target]
+                    first = shared if plane in (1, 2) else kept
                     for m in range(2):
-                        out[slot, j, plane, :, 128 * m : 128 * m + 128] = sums[
-                            j, plane, m, first : first + 64, :
+                        outs[slot][j, plane, :, 128 * m : 128 * m + 128] = sums[
+                            j, plane, m, pl.ds(first, 64), :
                         ].astype(jnp.bfloat16)
 
 
-def spectra(p, scal, seeing, own, far, dark, rate, ramp, wave, table):
-    n = own[0].shape[0]
-    frames = pl.BlockSpec((1, REGION, GROUP), lambda i, s: (i, 0, 0))
-    left = pl.BlockSpec((REGION, GROUP), lambda i, s: (0, p))
-    right = pl.BlockSpec((REGION, GROUP), lambda i, s: (0, p + 1))
+def spectra(first_sub, n_sub, tables, seeing, own, far, dark, rate, ramp, wave, table):
+    slabs = n_sub + 2
+    arrays = [a for a, c in own] + [a for a, c in far]
+    specs = [pl.BlockSpec((1, REGION, 128), lambda i, *s, c=c: (i, 0, c)) for a, c in own + far]
+    for const in (dark, rate):
+        arrays += [const] * slabs
+        specs += [
+            pl.BlockSpec((REGION, 128), lambda i, *s, c=first_sub + k: (0, c)) for k in range(slabs)
+        ]
+    arrays += [ramp[first_sub : first_sub + n_sub], wave, table]
+    specs += [
+        pl.BlockSpec((n_sub, S, REGION), lambda i, *s: (0, 0, 0)),
+        pl.BlockSpec(wave.shape, lambda i, *s: (0, 0, 0)),
+        pl.BlockSpec(table.shape, lambda i, *s: (0, 0)),
+    ]
+    part = (n_sub, 5, 64, S)
+    pairs = 8 * n_sub
     return pl.pallas_call(
-        spectra_kernel,
+        functools.partial(spectra_kernel, n_sub, first_sub),
         name="spectra",
         grid_spec=pltpu.PrefetchScalarGridSpec(
-            num_scalar_prefetch=1,
-            grid=(n,),
-            in_specs=[
-                pl.BlockSpec(memory_space=pltpu.SMEM),
-                frames,
-                frames,
-                frames,
-                frames,
-                left,
-                right,
-                left,
-                right,
-                pl.BlockSpec((2, S, REGION), lambda i, s: (p, 0, 0)),
-                pl.BlockSpec(wave.shape, lambda i, s: (0, 0, 0)),
-                pl.BlockSpec(table.shape, lambda i, s: (0, 0)),
-            ],
-            out_specs=pl.BlockSpec((4, 2, 5, 64, S), lambda i, s: (0, 0, 0, 0, 0)),
+            num_scalar_prefetch=4,
+            grid=(4,),
+            in_specs=[pl.BlockSpec(memory_space=pltpu.SMEM)] + specs,
+            out_specs=[pl.BlockSpec(part, lambda i, *s: (0, 0, 0, 0))] * 4,
             scratch_shapes=[
-                pltpu.VMEM((2, 4, REGION, 128), jnp.float32),
-                pltpu.VMEM((2, REGION, 2 * S), jnp.bfloat16),
-                pltpu.VMEM((2, 2, 2, HALF, 128), jnp.float32),
-                pltpu.VMEM((2, 2, 2, HALF, 128), jnp.float32),
-                pltpu.VMEM((2, 5, 2, HALF, 128), jnp.float32),
+                pltpu.VMEM((2, slabs, REGION, 128), jnp.float32),
+                pltpu.VMEM((n_sub, REGION, 2 * S), jnp.bfloat16),
+                pltpu.VMEM((2, n_sub, 2, HALF, 128), jnp.float32),
+                pltpu.VMEM((2, n_sub, 2, HALF, 128), jnp.float32),
+                pltpu.VMEM((n_sub, 5, 2, HALF, 128), jnp.float32),
             ],
         ),
-        out_shape=jax.ShapeDtypeStruct((4, 2, 5, 64, S), jnp.bfloat16),
+        out_shape=[jax.ShapeDtypeStruct(part, jnp.bfloat16)] * 4,
+        cost_estimate=pl.CostEstimate(
+            flops=pairs * 400_000_000, transcendentals=0, bytes_accessed=pairs * 1_000_000
+        ),
         compiler_params=pltpu.CompilerParams(
             dimension_semantics=("arbitrary",), vmem_limit_bytes=VMEM_LIMIT
         ),
-    )(scal, seeing, own[0], own[1], far[0], far[1], dark, dark, rate, rate, ramp, wave, table)
-
-
-def finish_kernel(mine, got1, got2, got3, flip, mix, inverse, *refs):
+    )(*tables, seeing, *arrays)
+
+
+def finish_kernel(n_sub, mine, got1, got2, got3, flip, mix, inverse, *refs):
     power, cross = refs[-2:]
-    for j in range(2):
+    for j in range(n_sub):
         for plane in range(5):
-            parts = jnp.concatenate([x[0, j, plane] for x in (mine, got1, got2, got3)], axis=0)
+            parts = jnp.concatenate([x[j, plane] for x in (mine, got1, got2, got3)], axis=0)
             turned = jnp.dot(
                 parts, flip[1 if plane >= 3 else 0], preferred_element_type=jnp.float32
             ).astype(jnp.bfloat16)
@@ -278,33 +281,33 @@
                 cross[j, plane - 1] = total
 
 
-def finish(p, parts, flip, mix, inverse, before, n_sub):
-    part = pl.BlockSpec((1, 2, 5, 64, S), lambda i: (0, 0, 0, 0, 0))
-    specs = [part] * 4 + [
-        pl.BlockSpec((2, S, S), lambda i: (0, 0, 0)),
-        pl.BlockSpec((64, S), lambda i: (0, 0)),
-        pl.BlockSpec((2, 1, S), lambda i: (p, 0, 0)),
-    ]
+def finish(first_sub, n_sub, parts, flip, mix, inverse, before, total_sub):
+    arrays = [*parts, flip, mix, inverse[first_sub : first_sub + n_sub]]
+    specs = [pl.BlockSpec(memory_space=pltpu.VMEM)] * 7
     aliases = {}
     if before is not None:
         specs += [pl.BlockSpec(memory_space=pl.ANY)] * 2
+        arrays += before
         aliases = {7: 0, 8: 1}
     return pl.pallas_call(
-        finish_kernel,
+        functools.partial(finish_kernel, n_sub),
         name="finish",
         grid=(1,),
         in_specs=specs,
         out_specs=[
-            pl.BlockSpec((2, 64, S), lambda i: (p, 0, 0)),
-            pl.BlockSpec((2, 4, 64, S), lambda i: (p, 0, 0, 0)),
+            pl.BlockSpec((pl.Element(n_sub), pl.Element(64), pl.Element(S)), lambda i: (first_sub, 0, 0)),
+            pl.BlockSpec(
+                (pl.Element(n_sub), pl.Element(4), pl.Element(64), pl.Element(S)),
+                lambda i: (first_sub, 0, 0, 0),
+            ),
         ],
         out_shape=[
-            jax.ShapeDtypeStruct((n_sub, 64, S), jnp.float32),
-            jax.ShapeDtypeStruct((n_sub, 4, 64, S), jnp.float32),
+            jax.ShapeDtypeStruct((total_sub, 64, S), jnp.float32),
+            jax.ShapeDtypeStruct((total_sub, 4, 64, S), jnp.float32),
         ],
         input_output_aliases=aliases,
         compiler_params=pltpu.CompilerParams(vmem_limit_bytes=VMEM_LIMIT),
-    )(*parts, flip, mix, inverse, *(before or ()))
+    )(*arrays)
 
 
 def local_rows(raw_frames, dark_frame, flat_field, seeing, anchors, taper):
@@ -312,71 +315,57 @@
     segment = lax.axis_index("segment")
     chip = tile // 2
     core = tile % 2
-    n_sub = seeing.shape[1]
-    width = raw_frames.shape[2]
-    n_groups = width // GROUP
+    total_sub = seeing.shape[1]
     frame = raw_frames[0]
 
-    def along(step):
-        return [(2 * z + k, 2 * (z + step) + k) for z in range(4) for k in range(2) if 0 <= z + step < 4]
-
-    def right(x):
-        return lax.ppermute(x, "tile", along(1))
-
-    def left(x):
-        return lax.ppermute(x, "tile", along(-1))
+    def send(x, to):
+        pairs = [(2 * z + k, to(z, k)) for z in range(4) for k in range(2)]
+        return lax.ppermute(x, "tile", pairs)
+
+    def beside(x):
+        return send(x, lambda z, k: 2 * (z ^ 1) + k)
+
+    def two_on(x):
+        return send(x, lambda z, k: 2 * ((z + 2) % 4) + k)
+
+    def opposite(x):
+        return send(x, lambda z, k: 2 * (3 - z) + k)
+
+    def inner(x):
+        return send(x, lambda z, k: 2 * (3 - z) + k if z in (1, 2) else 2 * z + 1 - k)
 
     def swap(x):
-        return lax.ppermute(x, "tile", [(t, t ^ 1) for t in range(8)])
-
-    own_rows = lax.dynamic_slice_in_dim(frame, 256 * chip, 512, 0)
-    cut = [slice(GROUP * g, GROUP * g + GROUP) for g in range(n_groups)]
-
-    gathered = []
-    gate_r = gate_l = None
-    for g in range(n_groups):
-        send_r = frame[768:1280, cut[g]]
-        send_l = frame[0:512, cut[g]]
-        if gate_r is not None:
-            send_r, gate_r = lax.optimization_barrier((send_r, gate_r))
-            send_l, gate_l = lax.optimization_barrier((send_l, gate_l))
-        r1 = right(send_r)
-        l1 = left(send_l)
-        gate_r, gate_l = r1, l1
-        r2 = right(jnp.where(chip == 0, frame[256:768, cut[g]], r1))
-        l2 = left(jnp.where(chip == 3, frame[512:1024, cut[g]], l1))
-        middle = frame[512:768, cut[g]]
-        r3 = right(jnp.where(chip == 1, jnp.concatenate([middle, r2[256:]], 0), r2))
-        l3 = left(jnp.where(chip == 2, jnp.concatenate([middle, l2[:256]], 0), l2))
-        own = own_rows[:, cut[g]]
-
-        def pick(a, b, c, d):
-            return jnp.where(chip == 0, a, jnp.where(chip == 1, b, jnp.where(chip == 2, c, d)))
-
-        def cat(a, b):
-            return jnp.concatenate([a, b], 0)
-
-        stack = jnp.stack(
-            [
-                pick(own, r2, cat(r3[256:], r2[:256]), r3),
-                pick(l1, own, cat(r3[:256], r1[:256]), r2),
-                pick(l2, cat(l1[256:], l3[:256]), own, r1),
-                pick(l3, cat(l2[256:], l3[256:]), l2, own),
-            ]
-        )
-        upper = stack[:, :REGION]
-        lower = stack[:, 128 : 128 + REGION]
-        keep = jnp.where(core == 0, upper, lower)
-        give = jnp.where(core == 0, lower, upper)
-        gathered.append((keep, swap(give)))
+        return send(x, lambda z, k: 2 * z + 1 - k)
+
+    def rows(first, length):
+        return lax.dynamic_slice_in_dim(frame, first, length, 0)
+
+    low = chip < 2
+    edge = (chip == 0) | (chip == 3)
+    to_beside = rows(256 * jnp.bitwise_xor(chip, 1), 512)
+    to_two_on = rows(jnp.where(chip == 0, 768, jnp.where(chip == 1, 1024, jnp.where(chip == 2, 0, 256))), 256)
+    to_opposite = rows(jnp.where(chip == 0, 1024, jnp.where(chip == 1, 768, jnp.where(chip == 2, 256, 0))), 256)
+    own_rows = rows(256 * chip, 512)
+
+    starts = []
+    start = 0
+    for blocks in COLUMN_BLOCKS:
+        cut = slice(128 * start, 128 * (start + blocks))
+        starts.append((start, cut))
+        start += blocks
+
+    first_hop = [
+        (beside(to_beside[:, cut]), two_on(to_two_on[:, cut]), opposite(to_opposite[:, cut]))
+        for start, cut in starts
+    ]
 
     first_row = 128 * tile
     dark = lax.dynamic_slice_in_dim(dark_frame, first_row, REGION, 0).astype(jnp.float32)
     rate = 1.0 / lax.dynamic_slice_in_dim(flat_field, first_row, REGION, 0).astype(jnp.float32)
-    mine = lax.dynamic_slice_in_dim(anchors, n_sub * tile, n_sub, 0)
-    widths = lax.dynamic_slice_in_dim(taper, n_sub * tile, n_sub, 0)
+    mine = lax.dynamic_slice_in_dim(anchors, total_sub * tile, total_sub, 0)
+    widths = lax.dynamic_slice_in_dim(taper, total_sub * tile, total_sub, 0)
     top = mine[:, 0] - first_row
-    side = mine[:, 1] - 128 * jnp.arange(n_sub, dtype=jnp.int32)
+    side = mine[:, 1] - 128 * jnp.arange(total_sub, dtype=jnp.int32)
     ramp = shifted_ramps(widths, jnp.zeros_like(side), S)[:, :, None] * shifted_ramps(
         widths, side, REGION
     )[:, None, :]
@@ -386,7 +375,7 @@
     wave = wave.reshape(2 * S, 4, 128).transpose(1, 0, 2)
     table = jnp.concatenate([cosine[:HALF], sine[:HALF]], axis=0)
     inverse = 1.0 / jnp.sum(seeing, axis=0)
-    inverse = jnp.broadcast_to(inverse[:, None, None], (n_sub, 1, S))
+    inverse = jnp.broadcast_to(inverse[:, None, None], (total_sub, 1, S))
     row = jnp.arange(S, dtype=jnp.int32)
     mirrored = segment >= 2
     turn = jnp.stack([(S - row) % S, S - 1 - row])
@@ -394,22 +383,48 @@
     flip = (turn[:, None, :] == row[None, :, None]).astype(jnp.bfloat16)
     order = jnp.where(mirrored, 63 - row[:64], row[:64])
     mix = (row[None, :] % 64 == order[:, None]).astype(jnp.bfloat16)
-
+    eight = jnp.arange(8, dtype=jnp.int32)
+    slot = eight % 4
+    source = jnp.where(slot == 1, jnp.bitwise_xor(chip, 1), chip)
+    source = jnp.where(slot == 2, (chip + 2) % 4, source)
+    source = jnp.where(slot == 3, 3 - chip, source)
+    frames = 8 * segment + 2 * source + jnp.where(eight < 4, core, 1 - core)
+    tables = (frames, top, side, jnp.where(eight == 0, segment, 0))
+
+    own_slabs = []
+    far_slabs = []
+    done = 0
     result = None
-    for p in range(n_groups - 1):
-        scal = jnp.concatenate(
-            [
-                jnp.stack([segment, 8 * segment, core, jnp.int32(2 * p)]),
-                jnp.stack([top[2 * p], side[2 * p], top[2 * p + 1], side[2 * p + 1]]),
-            ]
-        ).astype(jnp.int32)
-        own = (gathered[p][0], gathered[p + 1][0])
-        far = (gathered[p][1], gathered[p + 1][1])
-        partial = spectra(p, scal, seeing, own, far, dark, rate, ramp, wave, table)
-        parts = [partial[:1]]
-        for m in range(1, 4):
-            parts.append(lax.ppermute(partial[m : m + 1], "segment", [(s, s ^ m) for s in range(4)]))
-        result = finish(p, parts, flip, mix, inverse, result, n_sub)
+    gate = None
+    for g, (start, cut) in enumerate(starts):
+        near, two, far = first_hop[g]
+        if gate is not None:
+            near, two, far, gate = lax.optimization_barrier((near, two, far, gate))
+        f1 = beside(jnp.concatenate([far, two], 0))
+        passed = jnp.where(low, near[256:], near[:256])
+        f2 = inner(jnp.concatenate([passed, frame[512:768, cut]], 0))
+        f = jnp.where(edge, f1, f2)
+        two = jnp.where(low, jnp.concatenate([two, f[:256]], 0), jnp.concatenate([f[:256], two], 0))
+        far = jnp.where(low, jnp.concatenate([far, f[256:]], 0), jnp.concatenate([f[256:], far], 0))
+        stack = jnp.stack([own_rows[:, cut], near, two, far])
+        upper = stack[:, :REGION]
+        lower = stack[:, 128 : 128 + REGION]
+        keep = jnp.where(core == 0, upper, lower)
+        got = swap(jnp.where(core == 0, lower, upper))
+        for c in range(COLUMN_BLOCKS[g]):
+            own_slabs.append((keep, c))
+            far_slabs.append((got, c))
+        n_sub = len(own_slabs) - 2 - done
+        span = slice(done, done + n_sub + 2)
+        parts = spectra(
+            done, n_sub, tables, seeing, own_slabs[span], far_slabs[span], dark, rate, ramp, wave, table
+        )
+        gate = parts[0]
+        parts = [parts[0]] + [
+            lax.ppermute(parts[m], "segment", [(s, s ^ m) for s in range(4)]) for m in range(1, 4)
+        ]
+        result = finish(done, n_sub, parts, flip, mix, inverse, result, total_sub)
+        done += n_sub
     return tuple(result)
 
 

time: 278 us -> 249 us (0.90)
  starting transfers between devices: 95 us -> 49.3 us
  waiting for transfers between devices: 31.3 us -> 57.7 us
  local copies, waits for them, and re-layouts: 41.7 us -> 34.9 us
    ppermute x47 -> x36, starting transfers between devices: 95 us -> 49.3 us  [the longest x24 31.4 us: send(): return lax.ppermute(x, 'tile', pairs)]
    ppermute x47 -> x36, waiting for transfers between devices: 31.3 us -> 57.7 us  [the longest x24 40.7 us: send(): return lax.ppermute(x, 'tile', pairs)]
    concatenate x4, local copies, waits for them, and re-layouts: 12.7 us -> 0.11 us  [local_rows(): jnp.concatenate([two, f[:256]], 0)]
    another operation x14 -> x4, other arithmetic: 6.68 us -> 1.75 us  [local_rows(): stack = jnp.stack([own_rows[:, cut], near, two, far])]
    slice x44 -> x22, local copies, waits for them, and re-layouts: 19.4 us -> 20.5 us  [the longest x3 5.45 us: spectra(): arrays += [ramp[first_sub:first_sub + n_sub], wave, table]]
    select_n x13 -> x20, other arithmetic: 10.8 us -> 10.9 us  [the longest x4 4.91 us: local_rows(): got = swap(jnp.where(core == 0, lower, upper))]
    unnamed x99 -> x75, local copies, waits for them, and re-layouts: 5.91 us -> 5.97 us
  transfers between devices with their start and end apart: 47 -> 36, of which waited for: 17 -> 8; matrix products, arithmetic and copies ran while one was open for 25% -> 22% of each run, Pallas kernels for 24% -> 27%
where the time goes in v2:
time: 249 us; the launch traced here: 248 us
  Pallas kernels  71.3 us (29%)
  waiting for transfers between devices  57.7 us (23%)
  starting transfers between devices  49.3 us (20%)
  local copies, waits for them, and re-layouts  34.9 us (14%)
  other arithmetic  33.8 us (14%)
    pallas_call x4, Pallas kernels, spectra(): pl.pallas_call(functools.partial(spectra_kernel, n_sub, first_sub), name=...  53.3 us
    ppermute x24, waiting for transfers between devices, send(): return lax.ppermute(x, 'tile', pairs)  40.7 us
    ppermute x24, starting transfers between devices, send(): return lax.ppermute(x, 'tile', pairs)  31.4 us
    pallas_call x4, Pallas kernels, finish(): pl.pallas_call(functools.partial(finish_kernel, n_sub), name='finish', gr...  18 us
    ppermute x12, starting transfers between devices, local_rows(): lax.ppermute(parts[m], 'segment', [(s, s ^ m) for s in range(4)])  17.9 us
    ppermute x12, waiting for transfers between devices, local_rows(): lax.ppermute(parts[m], 'segment', [(s, s ^ m) for s in range(4)])  16.9 us
    unnamed x75, local copies, waits for them, and re-layouts  5.97 us
    slice x3, local copies, waits for them, and re-layouts, spectra(): arrays += [ramp[first_sub:first_sub + n_sub], wave, table]  5.45 us
  transfers between devices with their start and end apart: 36, of which 8 were waited for; matrix products, arithmetic and copies ran while one was open for 22% of the time, Pallas kernels for 27%

profile of v2, /device:TPU:0, one launch (start us, length us, event | category | flops | bytes accessed | tf_op | source)
XLA Modules:
  0.0 248.3 jit_solution(3246923636420822536)
XLA Ops:
  3.0 4.0 %collective-permute-start.9 = (bf16[256,384]{1,0:T(8,128)(2,1)}, bf16[256,384]{1,0:T(8,128)(2,1)}, u32[]{:S(2)}, u32[]{:S(2)}) collective-permute-start(bf16[256,384]{1,0:T(8,128)(2,1)} %slice.282), channel_id=1, source_target_pairs={{0,4},{1,5},{2,6},{3,7},{4,0},{5,1},{6,2},{7,3},{8,12},{9,13},{10,... | collective-permute-start | bytes 589832 | tf_op jit(solution)/shard_map/ppermute | solution.py:323
  30.2 12.5 %collective-permute-done.4 = bf16[256,512]{1,0:T(8,128)(2,1)} collective-permute-done((bf16[256,512]{1,0:T(8,128)(2,1)}, bf16[256,512]{1,0:T(8,128)(2,1)}, u32[]{:S(2)}, u32[]{:S(2)}) %collective-permute-start.4) | collective-permute-done | bytes 262176 | tf_op jit(solution)/shard_map/ppermute | solution.py:323
  43.8 5.6 %collective-permute-start.6 = (bf16[512,512]{1,0:T(8,128)(2,1)S(1)}, bf16[512,512]{1,0:T(8,128)(2,1)S(1)}, u32[]{:S(2)}, u32[]{:S(2)}) collective-permute-start(bf16[512,512]{1,0:T(8,128)(2,1)S(1)} %pad_maximum_fusion.4), channel_id=1, source_target_pairs={{0,2},{1,3},{2,0},{3,1},{4,6},{5,7},{6,4},{7,5},{8,10},{9,11},{10,... | collective-permute-start | bytes 1572872 | tf_op jit(solution)/shard_map/ppermute | solution.py:323
  50.9 12.8 %collective-permute-done.6 = bf16[512,512]{1,0:T(8,128)(2,1)S(1)} collective-permute-done((bf16[512,512]{1,0:T(8,128)(2,1)S(1)}, bf16[512,512]{1,0:T(8,128)(2,1)S(1)}, u32[]{:S(2)}, u32[]{:S(2)}) %collective-permute-start.6) | collective-permute-done | bytes 524320 | tf_op jit(solution)/shard_map/ppermute | solution.py:323
  76.3 2.6 %dynamic-slice_convert_fusion.refs_8_.refs_9_.refs_10_.refs_11_.refs_12_.refs_13_.refs_14_.refs_6_.refs_7_ = f32[384,1280]{1,0:T(8,128)} fusion(bf16[1280,1280]{1,0:T(8,128)(2,1)} %param.7, s32[]{:T(128)S(6)} %select_n.419), kind=kLoop, calls=%fused_computation.15 | loop fusion | flops 491520 | bytes 2949124 | tf_op jit(solution)/shard_map/convert_element_type | solution.py:363
  78.9 2.8 %convert_divide_fusion.refs_12_.refs_13_.refs_14_.refs_15_.refs_16_.refs_17_.refs_18_.refs_19_.refs_9_.refs_10_.refs_11_ = f32[384,1280]{1,0:T(8,128)} fusion(bf16[1280,1280]{1,0:T(8,128)(2,1)} %param.8, s32[]{:T(128)S(6)} %select_n.419), kind=kLoop, calls=%fused_computation.1 | loop fusion | flops 983040 | bytes 2949124 | tf_op jit(solution)/shard_map/div | solution.py:364
  83.0 13.5 %spectra.4 = (bf16[2,5,64,256]{3,2,1,0:T(8,128)(2,1)}, bf16[2,5,64,256]{3,2,1,0:T(8,128)(2,1)}, bf16[2,5,64,256]{3,2,1,0:T(8,128)(2,1)}, bf16[2,5,64,256]{3,2,1,0:T(8,128)(2,1)}) custom-call(s32[8]{0:T(128)} %get-tuple-element.91.frames, s32[8]{0:T(128)} %get-tuple-element.87.tops, s32[8]{0:T(128)} %bitcast_subtract_fusion.sides, s32[8]{0:T(128)} %get-tuple-element.90.spot, ...), custom_call_target="tpu_custom_call" | custom-call | flops 6400000000 | bytes 16000000 | tf_op jit(solution)/shard_map/spectra/pallas_call | solution.py:242
  97.6 2.7 %collective-permute-start.12 = (bf16[512,384]{1,0:T(8,128)(2,1)S(1)}, bf16[512,384]{1,0:T(8,128)(2,1)S(1)}, u32[]{:S(2)}, u32[]{:S(2)}) collective-permute-start(bf16[512,384]{1,0:T(8,128)(2,1)S(1)} %pad_maximum_fusion.7), channel_id=1, source_target_pairs={{0,2},{1,3},{2,0},{3,1},{4,6},{5,7},{6,4},{7,5},{8,10},{9,11},{10,... | collective-permute-start | bytes 1179656 | tf_op jit(solution)/shard_map/ppermute | solution.py:323
  100.7 9.4 %collective-permute-done.12 = bf16[512,384]{1,0:T(8,128)(2,1)S(1)} collective-permute-done((bf16[512,384]{1,0:T(8,128)(2,1)S(1)}, bf16[512,384]{1,0:T(8,128)(2,1)S(1)}, u32[]{:S(2)}, u32[]{:S(2)}) %collective-permute-start.12) | collective-permute-done | bytes 393248 | tf_op jit(solution)/shard_map/ppermute | solution.py:323
  114.9 3.9 %collective-permute-start.1 = (bf16[256,256]{1,0:T(8,128)(2,1)S(1)}, bf16[256,256]{1,0:T(8,128)(2,1)S(1)}, u32[]{:S(2)}, u32[]{:S(2)}) collective-permute-start(bf16[256,256]{1,0:T(8,128)(2,1)S(1)} %slice.267), channel_id=1, source_target_pairs={{0,4},{1,5},{2,6},{3,7},{4,0},{5,1},{6,2},{7,3},{8,12},{9,13},{10,... | collective-permute-start | bytes 393224 | tf_op jit(solution)/shard_map/ppermute | solution.py:323
  126.3 17.3 %spectra.5 = (bf16[3,5,64,256]{3,2,1,0:T(8,128)(2,1)}, bf16[3,5,64,256]{3,2,1,0:T(8,128)(2,1)}, bf16[3,5,64,256]{3,2,1,0:T(8,128)(2,1)}, bf16[3,5,64,256]{3,2,1,0:T(8,128)(2,1)}) custom-call(s32[8]{0:T(128)} %get-tuple-element.91.frames, s32[8]{0:T(128)} %get-tuple-element.87.tops, s32[8]{0:T(128)} %bitcast_subtract_fusion.sides, s32[8]{0:T(128)} %get-tuple-element.90.spot, ...), custom_call_target="tpu_custom_call" | custom-call | flops 9600000000 | bytes 24000000 | tf_op jit(solution)/shard_map/spectra/pallas_call | solution.py:242
  145.9 6.1 %collective-permute-done.15 = bf16[512,256]{1,0:T(8,128)(2,1)S(1)} collective-permute-done((bf16[512,256]{1,0:T(8,128)(2,1)S(1)}, bf16[512,256]{1,0:T(8,128)(2,1)S(1)}, u32[]{:S(2)}, u32[]{:S(2)}) %collective-permute-start.15) | collective-permute-done | bytes 262176 | tf_op jit(solution)/shard_map/ppermute | solution.py:323
  154.3 2.9 %collective-permute-start.18 = (bf16[256,128]{1,0:T(8,128)(2,1)S(1)}, bf16[256,128]{1,0:T(8,128)(2,1)S(1)}, u32[]{:S(2)}, u32[]{:S(2)}) collective-permute-start(bf16[256,128]{1,0:T(8,128)(2,1)S(1)} %slice.301), channel_id=1, source_target_pairs={{0,4},{1,5},{2,6},{3,7},{4,0},{5,1},{6,2},{7,3},{8,12},{9,13},{10,... | collective-permute-start | bytes 196616 | tf_op jit(solution)/shard_map/ppermute | solution.py:323
  162.9 13.2 %spectra.6 = (bf16[2,5,64,256]{3,2,1,0:T(8,128)(2,1)}, bf16[2,5,64,256]{3,2,1,0:T(8,128)(2,1)}, bf16[2,5,64,256]{3,2,1,0:T(8,128)(2,1)}, bf16[2,5,64,256]{3,2,1,0:T(8,128)(2,1)}) custom-call(s32[8]{0:T(128)} %get-tuple-element.91.frames, s32[8]{0:T(128)} %get-tuple-element.87.tops, s32[8]{0:T(128)} %bitcast_subtract_fusion.sides, s32[8]{0:T(128)} %get-tuple-element.90.spot, ...), custom_call_target="tpu_custom_call" | custom-call | flops 6400000000 | bytes 16000000 | tf_op jit(solution)/shard_map/spectra/pallas_call | solution.py:242
  185.2 4.0 %collective-permute-done.33.got1 = bf16[2,5,64,256]{3,2,1,0:T(8,128)(2,1)S(1)} collective-permute-done((bf16[2,5,64,256]{3,2,1,0:T(8,128)(2,1)}, bf16[2,5,64,256]{3,2,1,0:T(8,128)(2,1)S(1)}, u32[]{:S(2)}, u32[]{:S(2)}) %collective-permute-start.33) | collective-permute-done | bytes 327712 | tf_op jit(solution)/shard_map/ppermute | solution.py:424
  190.8 6.3 %collective-permute-done.34.got2 = bf16[2,5,64,256]{3,2,1,0:T(8,128)(2,1)S(1)} collective-permute-done((bf16[2,5,64,256]{3,2,1,0:T(8,128)(2,1)}, bf16[2,5,64,256]{3,2,1,0:T(8,128)(2,1)S(1)}, u32[]{:S(2)}, u32[]{:S(2)}) %collective-permute-start.34) | collective-permute-done | bytes 327712 | tf_op jit(solution)/shard_map/ppermute | solution.py:424
  203.2 3.6 %collective-permute-done.30.got1 = bf16[3,5,64,256]{3,2,1,0:T(8,128)(2,1)S(1)} collective-permute-done((bf16[3,5,64,256]{3,2,1,0:T(8,128)(2,1)}, bf16[3,5,64,256]{3,2,1,0:T(8,128)(2,1)S(1)}, u32[]{:S(2)}, u32[]{:S(2)}) %collective-permute-start.30) | collective-permute-done | bytes 491552 | tf_op jit(solution)/shard_map/ppermute | solution.py:424
  209.9 9.4 %spectra.7 = (bf16[1,5,64,256]{3,2,1,0:T(8,128)(2,1)}, bf16[1,5,64,256]{3,2,1,0:T(8,128)(2,1)}, bf16[1,5,64,256]{3,2,1,0:T(8,128)(2,1)}, bf16[1,5,64,256]{3,2,1,0:T(8,128)(2,1)}) custom-call(s32[8]{0:T(128)} %get-tuple-element.91.frames, s32[8]{0:T(128)} %get-tuple-element.87.tops, s32[8]{0:T(128)} %bitcast_subtract_fusion.sides, s32[8]{0:T(128)} %get-tuple-element.90.spot, ...), custom_call_target="tpu_custom_call" | custom-call | flops 3200000000 | bytes 8000000 | tf_op jit(solution)/shard_map/spectra/pallas_call | solution.py:242
  221.5 3.0 %collective-permute-done.27.got1 = bf16[2,5,64,256]{3,2,1,0:T(8,128)(2,1)S(1)} collective-permute-done((bf16[2,5,64,256]{3,2,1,0:T(8,128)(2,1)}, bf16[2,5,64,256]{3,2,1,0:T(8,128)(2,1)S(1)}, u32[]{:S(2)}, u32[]{:S(2)}) %collective-permute-start.27) | collective-permute-done | bytes 327712 | tf_op jit(solution)/shard_map/ppermute | solution.py:424
  224.5 2.5 collective-permute-start.26
  227.6 4.5 %finish.4 = (f32[8,64,256]{2,1,0:T(8,128)}, f32[8,4,64,256]{3,2,1,0:T(8,128)}) custom-call(bf16[2,5,64,256]{3,2,1,0:T(8,128)(2,1)} %get-tuple-element.33.mine, bf16[2,5,64,256]{3,2,1,0:T(8,128)(2,1)} %copy-done.16, bf16[2,5,64,256]{3,2,1,0:T(8,128)(2,1)} %copy-done.17, bf16[2,5,64,256]{3,2,1,0:T(8,128)(2,1)} %copy-done.18, bf16[2,256,256]{2,1,0:T(8,128)(2,1)} %fusion.2.flip, ...), custom_call_target="tpu_custom_call" | custom-call | tf_op jit(solution)/shard_map/finish/pallas_call | solution.py:292
  232.8 5.8 %finish.5 = (f32[8,64,256]{2,1,0:T(8,128)}, f32[8,4,64,256]{3,2,1,0:T(8,128)}) custom-call(bf16[3,5,64,256]{3,2,1,0:T(8,128)(2,1)} %get-tuple-element.37.mine, bf16[3,5,64,256]{3,2,1,0:T(8,128)(2,1)} %copy-done.12, bf16[3,5,64,256]{3,2,1,0:T(8,128)(2,1)} %copy-done.13, ...), custom_call_target="tpu_custom_call", output_to_operand_aliasing={{0}: (7, {}), {1}: (8, {})} | custom-call | tf_op jit(solution)/shard_map/finish/pallas_call | solution.py:292
  239.5 4.5 %finish.6 = (f32[8,64,256]{2,1,0:T(8,128)}, f32[8,4,64,256]{3,2,1,0:T(8,128)}) custom-call(bf16[2,5,64,256]{3,2,1,0:T(8,128)(2,1)} %get-tuple-element.41.mine, bf16[2,5,64,256]{3,2,1,0:T(8,128)(2,1)} %copy-done.19, bf16[2,5,64,256]{3,2,1,0:T(8,128)(2,1)} %copy-done.20, ...), custom_call_target="tpu_custom_call", output_to_operand_aliasing={{0}: (7, {}), {1}: (8, {})} | custom-call | tf_op jit(solution)/shard_map/finish/pallas_call | solution.py:292
  245.1 3.2 %finish.7 = (f32[8,64,256]{2,1,0:T(8,128)}, f32[8,4,64,256]{3,2,1,0:T(8,128)}) custom-call(bf16[1,5,64,256]{3,2,1,0:T(8,128)(2,1)} %get-tuple-element.45.mine, bf16[1,5,64,256]{3,2,1,0:T(8,128)(2,1)} %copy-done.22, bf16[1,5,64,256]{3,2,1,0:T(8,128)(2,1)} %copy-done.23, ...), custom_call_target="tpu_custom_call", output_to_operand_aliasing={{0}: (7, {}), {1}: (8, {})} | custom-call | tf_op jit(solution)/shard_map/finish/pallas_call | solution.py:292
  (230 shorter events, 91.2 us)
Async XLA Ops:
  3.0 93.4 %collective-permute-start.9 = (bf16[256,384]{1,0:T(8,128)(2,1)}, bf16[256,384]{1,0:T(8,128)(2,1)}, u32[]{:S(2)}, u32[]{:S(2)}) collective-permute-start(bf16[256,384]{1,0:T(8,128)(2,1)} %slice.282), channel_id=1, source_target_pairs={{0,4},{1,5},{2,6},{3,7},{4,0},{5,1},{6,2},{7,3},{8,12},{9,13},{10,... | collective-permute-start | bytes 589832 | tf_op jit(solution)/shard_map/ppermute | solution.py:323
  7.7 88.7 %collective-permute-start.10 = (bf16[256,384]{1,0:T(8,128)(2,1)}, bf16[256,384]{1,0:T(8,128)(2,1)}, u32[]{:S(2)}, u32[]{:S(2)}) collective-permute-start(bf16[256,384]{1,0:T(8,128)(2,1)} %slice.283), channel_id=1, source_target_pairs={{0,6},{1,7},{2,4},{3,5},{4,2},{5,3},{6,0},{7,1},{8,14},{9,15},{10,... | collective-permute-start | bytes 589832 | tf_op jit(solution)/shard_map/ppermute | solution.py:323
  9.8 32.9 %collective-permute-start.4 = (bf16[256,512]{1,0:T(8,128)(2,1)}, bf16[256,512]{1,0:T(8,128)(2,1)}, u32[]{:S(2)}, u32[]{:S(2)}) collective-permute-start(bf16[256,512]{1,0:T(8,128)(2,1)} %slice.271), channel_id=1, source_target_pairs={{0,4},{1,5},{2,6},{3,7},{4,0},{5,1},{6,2},{7,3},{8,12},{9,13},{10,... | collective-permute-start | bytes 786440 | tf_op jit(solution)/shard_map/ppermute | solution.py:323
  12.3 30.4 %collective-permute-start.5 = (bf16[256,512]{1,0:T(8,128)(2,1)}, bf16[256,512]{1,0:T(8,128)(2,1)}, u32[]{:S(2)}, u32[]{:S(2)}) collective-permute-start(bf16[256,512]{1,0:T(8,128)(2,1)} %slice.272), channel_id=1, source_target_pairs={{0,6},{1,7},{2,4},{3,5},{4,2},{5,3},{6,0},{7,1},{8,14},{9,15},{10,... | collective-permute-start | bytes 786440 | tf_op jit(solution)/shard_map/ppermute | solution.py:323
  16.3 33.1 %collective-permute-start.3 = (bf16[512,512]{1,0:T(8,128)(2,1)}, bf16[512,512]{1,0:T(8,128)(2,1)}, u32[]{:S(2)}, u32[]{:S(2)}) collective-permute-start(bf16[512,512]{1,0:T(8,128)(2,1)} %slice.270), channel_id=1, source_target_pairs={{0,2},{1,3},{2,0},{3,1},{4,6},{5,7},{6,4},{7,5},{8,10},{9,11},{10,... | collective-permute-start | bytes 1572872 | tf_op jit(solution)/shard_map/ppermute | solution.py:323
  42.7 53.8 %collective-permute-start.8 = (bf16[512,384]{1,0:T(8,128)(2,1)}, bf16[512,384]{1,0:T(8,128)(2,1)S(1)}, u32[]{:S(2)}, u32[]{:S(2)}) collective-permute-start(bf16[512,384]{1,0:T(8,128)(2,1)} %slice.281), channel_id=1, source_target_pairs={{0,2},{1,3},{2,0},{3,1},{4,6},{5,7},{6,4},{7,5},{8,10},{9,11},{10,... | collective-permute-start | bytes 1179656 | tf_op jit(solution)/shard_map/ppermute | solution.py:323
  43.8 19.8 %collective-permute-start.6 = (bf16[512,512]{1,0:T(8,128)(2,1)S(1)}, bf16[512,512]{1,0:T(8,128)(2,1)S(1)}, u32[]{:S(2)}, u32[]{:S(2)}) collective-permute-start(bf16[512,512]{1,0:T(8,128)(2,1)S(1)} %pad_maximum_fusion.4), channel_id=1, source_target_pairs={{0,2},{1,3},{2,0},{3,1},{4,6},{5,7},{6,4},{7,5},{8,10},{9,11},{10,... | collective-permute-start | bytes 1572872 | tf_op jit(solution)/shard_map/ppermute | solution.py:323
  114.9 28.8 %collective-permute-start.1 = (bf16[256,256]{1,0:T(8,128)(2,1)S(1)}, bf16[256,256]{1,0:T(8,128)(2,1)S(1)}, u32[]{:S(2)}, u32[]{:S(2)}) collective-permute-start(bf16[256,256]{1,0:T(8,128)(2,1)S(1)} %slice.267), channel_id=1, source_target_pairs={{0,4},{1,5},{2,6},{3,7},{4,0},{5,1},{6,2},{7,3},{8,12},{9,13},{10,... | collective-permute-start | bytes 393224 | tf_op jit(solution)/shard_map/ppermute | solution.py:323
  119.7 24.0 %collective-permute-start.2 = (bf16[256,256]{1,0:T(8,128)(2,1)S(1)}, bf16[256,256]{1,0:T(8,128)(2,1)S(1)}, u32[]{:S(2)}, u32[]{:S(2)}) collective-permute-start(bf16[256,256]{1,0:T(8,128)(2,1)S(1)} %slice.268), channel_id=1, source_target_pairs={{0,6},{1,7},{2,4},{3,5},{4,2},{5,3},{6,0},{7,1},{8,14},{9,15},{10,... | collective-permute-start | bytes 393224 | tf_op jit(solution)/shard_map/ppermute | solution.py:323
  121.9 21.8 %collective-permute-start = (bf16[512,256]{1,0:T(8,128)(2,1)S(1)}, bf16[512,256]{1,0:T(8,128)(2,1)S(1)}, u32[]{:S(2)}, u32[]{:S(2)}) collective-permute-start(bf16[512,256]{1,0:T(8,128)(2,1)S(1)} %slice.266), channel_id=1, source_target_pairs={{0,2},{1,3},{2,0},{3,1},{4,6},{5,7},{6,4},{7,5},{8,10},{9,11},{10,... | collective-permute-start | bytes 786440 | tf_op jit(solution)/shard_map/ppermute | solution.py:323
  154.3 21.8 %collective-permute-start.18 = (bf16[256,128]{1,0:T(8,128)(2,1)S(1)}, bf16[256,128]{1,0:T(8,128)(2,1)S(1)}, u32[]{:S(2)}, u32[]{:S(2)}) collective-permute-start(bf16[256,128]{1,0:T(8,128)(2,1)S(1)} %slice.301), channel_id=1, source_target_pairs={{0,4},{1,5},{2,6},{3,7},{4,0},{5,1},{6,2},{7,3},{8,12},{9,13},{10,... | collective-permute-start | bytes 196616 | tf_op jit(solution)/shard_map/ppermute | solution.py:323
  158.0 18.0 %collective-permute-start.19 = (bf16[256,128]{1,0:T(8,128)(2,1)S(1)}, bf16[256,128]{1,0:T(8,128)(2,1)S(1)}, u32[]{:S(2)}, u32[]{:S(2)}) collective-permute-start(bf16[256,128]{1,0:T(8,128)(2,1)S(1)} %slice.302), channel_id=1, source_target_pairs={{0,6},{1,7},{2,4},{3,5},{4,2},{5,3},{6,0},{7,1},{8,14},{9,15},{10,... | collective-permute-start | bytes 196616 | tf_op jit(solution)/shard_map/ppermute | solution.py:323
  180.0 17.0 %collective-permute-start.34 = (bf16[2,5,64,256]{3,2,1,0:T(8,128)(2,1)}, bf16[2,5,64,256]{3,2,1,0:T(8,128)(2,1)S(1)}, u32[]{:S(2)}, u32[]{:S(2)}) collective-permute-start(bf16[2,5,64,256]{3,2,1,0:T(8,128)(2,1)} %get-tuple-element.56), channel_id=1, source_target_pairs={{0,16},{8,24},{16,0},{24,8},{1,17},{9,25},{17,1},{25,9},{2,18},{10... | collective-permute-start | bytes 983048 | tf_op jit(solution)/shard_map/ppermute | solution.py:424
  181.6 17.2 %collective-permute-start.35 = (bf16[2,5,64,256]{3,2,1,0:T(8,128)(2,1)}, bf16[2,5,64,256]{3,2,1,0:T(8,128)(2,1)S(1)}, u32[]{:S(2)}, u32[]{:S(2)}) collective-permute-start(bf16[2,5,64,256]{3,2,1,0:T(8,128)(2,1)} %get-tuple-element.57), channel_id=1, source_target_pairs={{0,24},{8,16},{16,8},{24,0},{1,25},{9,17},{17,9},{25,1},{2,26},{10... | collective-permute-start | bytes 983048 | tf_op jit(solution)/shard_map/ppermute | solution.py:424
  182.0 24.8 %collective-permute-start.30 = (bf16[3,5,64,256]{3,2,1,0:T(8,128)(2,1)}, bf16[3,5,64,256]{3,2,1,0:T(8,128)(2,1)S(1)}, u32[]{:S(2)}, u32[]{:S(2)}) collective-permute-start(bf16[3,5,64,256]{3,2,1,0:T(8,128)(2,1)} %get-tuple-element.52), channel_id=1, source_target_pairs={{0,8},{8,0},{16,24},{24,16},{1,9},{9,1},{17,25},{25,17},{2,10},{10... | collective-permute-start | bytes 1474568 | tf_op jit(solution)/shard_map/ppermute | solution.py:424
  184.6 23.8 %collective-permute-start.23 = (bf16[4,384,128]{2,1,0:T(8,128)(2,1)S(1)}, bf16[4,384,128]{2,1,0:T(8,128)(2,1)S(1)}, u32[]{:S(2)}, u32[]{:S(2)}) collective-permute-start(bf16[4,384,128]{2,1,0:T(8,128)(2,1)S(1)} %get-tuple-element.76), channel_id=1, source_target_pairs={{0,1},{1,0},{2,3},{3,2},{4,5},{5,4},{6,7},{7,6},{8,9},{9,8},{10,11... | collective-permute-start | bytes 1179656 | tf_op jit(solution)/shard_map/ppermute | solution.py:323
  189.3 30.1 %collective-permute-start.31 = (bf16[3,5,64,256]{3,2,1,0:T(8,128)(2,1)S(1)}, bf16[3,5,64,256]{3,2,1,0:T(8,128)(2,1)S(1)}, u32[]{:S(2)}, u32[]{:S(2)}) collective-permute-start(bf16[3,5,64,256]{3,2,1,0:T(8,128)(2,1)S(1)} %copy-done.34), channel_id=1, source_target_pairs={{0,16},{8,24},{16,0},{24,8},{1,17},{9,25},{17,1},{25,9},{2,18},{10... | collective-permute-start | bytes 1474568 | tf_op jit(solution)/shard_map/ppermute | solution.py:424
  197.1 23.1 %collective-permute-start.32 = (bf16[3,5,64,256]{3,2,1,0:T(8,128)(2,1)S(1)}, bf16[3,5,64,256]{3,2,1,0:T(8,128)(2,1)S(1)}, u32[]{:S(2)}, u32[]{:S(2)}) collective-permute-start(bf16[3,5,64,256]{3,2,1,0:T(8,128)(2,1)S(1)} %copy-done.33), channel_id=1, source_target_pairs={{0,24},{8,16},{16,8},{24,0},{1,25},{9,17},{17,9},{25,1},{2,26},{10... | collective-permute-start | bytes 1474568 | tf_op jit(solution)/shard_map/ppermute | solution.py:424
  198.7 25.7 %collective-permute-start.27 = (bf16[2,5,64,256]{3,2,1,0:T(8,128)(2,1)}, bf16[2,5,64,256]{3,2,1,0:T(8,128)(2,1)S(1)}, u32[]{:S(2)}, u32[]{:S(2)}) collective-permute-start(bf16[2,5,64,256]{3,2,1,0:T(8,128)(2,1)} %get-tuple-element.49), channel_id=1, source_target_pairs={{0,8},{8,0},{16,24},{24,16},{1,9},{9,1},{17,25},{25,17},{2,10},{10... | collective-permute-start | bytes 983048 | tf_op jit(solution)/shard_map/ppermute | solution.py:424
  206.9 31.8 %collective-permute-start.28 = (bf16[2,5,64,256]{3,2,1,0:T(8,128)(2,1)}, bf16[2,5,64,256]{3,2,1,0:T(8,128)(2,1)S(1)}, u32[]{:S(2)}, u32[]{:S(2)}) collective-permute-start(bf16[2,5,64,256]{3,2,1,0:T(8,128)(2,1)} %get-tuple-element.50), channel_id=1, source_target_pairs={{0,16},{8,24},{16,0},{24,8},{1,17},{9,25},{17,1},{25,9},{2,18},{10... | collective-permute-start | bytes 983048 | tf_op jit(solution)/shard_map/ppermute | solution.py:424
  208.4 30.3 %collective-permute-start.29 = (bf16[2,5,64,256]{3,2,1,0:T(8,128)(2,1)S(1)}, bf16[2,5,64,256]{3,2,1,0:T(8,128)(2,1)S(1)}, u32[]{:S(2)}, u32[]{:S(2)}) collective-permute-start(bf16[2,5,64,256]{3,2,1,0:T(8,128)(2,1)S(1)} %copy-done.35), channel_id=1, source_target_pairs={{0,24},{8,16},{16,8},{24,0},{1,25},{9,17},{17,9},{25,1},{2,26},{10... | collective-permute-start | bytes 983048 | tf_op jit(solution)/shard_map/ppermute | solution.py:424
  219.3 24.6 %collective-permute-start.24 = (bf16[1,5,64,256]{3,2,1,0:T(8,128)(2,1)}, bf16[1,5,64,256]{3,2,1,0:T(8,128)(2,1)S(1)}, u32[]{:S(2)}, u32[]{:S(2)}) collective-permute-start(bf16[1,5,64,256]{3,2,1,0:T(8,128)(2,1)} %get-tuple-element.46), channel_id=1, source_target_pairs={{0,8},{8,0},{16,24},{24,16},{1,9},{9,1},{17,25},{25,17},{2,10},{10... | collective-permute-start | bytes 491528 | tf_op jit(solution)/shard_map/ppermute | solution.py:424
  220.1 23.8 %collective-permute-start.25 = (bf16[1,5,64,256]{3,2,1,0:T(8,128)(2,1)}, bf16[1,5,64,256]{3,2,1,0:T(8,128)(2,1)S(1)}, u32[]{:S(2)}, u32[]{:S(2)}) collective-permute-start(bf16[1,5,64,256]{3,2,1,0:T(8,128)(2,1)} %get-tuple-element.47), channel_id=1, source_target_pairs={{0,16},{8,24},{16,0},{24,8},{1,17},{9,25},{17,1},{25,9},{2,18},{10... | collective-permute-start | bytes 491528 | tf_op jit(solution)/shard_map/ppermute | solution.py:424
  224.5 19.5 %collective-permute-start.26 = (bf16[1,5,64,256]{3,2,1,0:T(8,128)(2,1)}, bf16[1,5,64,256]{3,2,1,0:T(8,128)(2,1)S(1)}, u32[]{:S(2)}, u32[]{:S(2)}) collective-permute-start(bf16[1,5,64,256]{3,2,1,0:T(8,128)(2,1)} %get-tuple-element.48), channel_id=1, source_target_pairs={{0,24},{8,16},{16,8},{24,0},{1,25},{9,17},{17,9},{25,1},{2,26},{10... | collective-permute-start | bytes 491528 | tf_op jit(solution)/shard_map/ppermute | solution.py:424
  (50 other events, 454.2 us)
